TPU v7x, 128 devices: a whole 4x4x4 slice. The times are simulated.
128 devices in a mesh: ctx: 32 (over z, x_hi, y), tp: 4 (over x_lo, core).
Axes of the slice: x: 4 (x_hi: 2, x_lo: 2; x = x_hi * 2 + x_lo), y: 4, z: 4, core: 2. Of those that a mesh axis runs over, the one named last changes fastest.
Arguments:
- queries: bfloat16 [16384, 4096], P('ctx', 'tp'), may hold values from -6 to 6
- keys: bfloat16 [16384, 512], P('ctx', 'tp'), may hold values from -6 to 6
- values: bfloat16 [16384, 512], P('ctx', 'tp'), may hold values from -6 to 6
- out_weight: bfloat16 [4096, 8192], P('tp'), may hold values from -0.75 to 0.75
- vertical: int32 [32, 16], P('tp'), may hold values from 0 to 255, as said below
- slash: int32 [32, 8], P('tp'), may hold values from 0 to 15, as said below
Outputs:
- projected: bfloat16 [16384, 8192], P(('ctx', 'tp'))
Inputs may be any that keep to these rules, and one draw needn't show every extreme that they name: `vertical`: each head's 16 blocks are distinct. For each index of tp, the blocks named by its 8 heads include at most 2 blocks of any one ctx shard of 512 tokens, and exactly 2 of some shard. `slash`: each head's first offset is 0 and its 8 offsets are distinct.
All inputs are finite; a program needn't handle non-finite values.
Results may differ from a plain program's by a relative error of at most 0.013.
Values may be sent and summed in bfloat16 or wider, within the bound.
A program may use at most 128 MiB of HBM per device.

v0:
```python
import jax
import jax.numpy as jnp
from jax import lax
from jax.sharding import PartitionSpec as P

HS = 128
BLK = 64


def slot_table(vert_row, slash_row, query_blocks):
    block_count = query_blocks.shape[0]
    column_ids = query_blocks[:, None]
    vert_blocks = jnp.broadcast_to(vert_row[None, :], (block_count, vert_row.shape[0]))
    vert_ok = vert_blocks <= column_ids
    slash_blocks = column_ids - slash_row[None, :]
    repeated = jnp.any(slash_blocks[:, :, None] == vert_row[None, None, :], axis=2)
    slash_ok = (slash_blocks >= 0) & jnp.logical_not(repeated)
    blocks = jnp.concatenate([vert_blocks, slash_blocks], axis=1)
    usable = jnp.concatenate([vert_ok, slash_ok], axis=1)
    return (blocks, usable)


def attend(head_query, key_tiles, value_tiles, blocks, usable, query_blocks):
    block_len = head_query.shape[1]
    score_scale = 1.0 / jnp.sqrt(jnp.float32(head_query.shape[2]))
    scores = (
        jnp.einsum("ibd,isjd->ibsj", head_query, key_tiles, preferred_element_type=jnp.float32)
        * score_scale
    )
    diagonal = blocks == query_blocks[:, None]
    positions = jnp.arange(block_len, dtype=jnp.int32)
    above_diag = positions[None, :] > positions[:, None]
    blocked = (
        jnp.logical_not(usable)[:, None, :, None]
        | diagonal[:, None, :, None] & above_diag[None, :, None, :]
    )
    scores = jnp.where(blocked, jnp.float32(-1e30), scores)
    row_max = jnp.max(scores, axis=(2, 3), keepdims=True)
    weights = jnp.exp(scores - row_max)
    row_total = jnp.sum(weights, axis=(2, 3))
    rounded_probs = weights.astype(jnp.bfloat16)
    attended = jnp.einsum(
        "ibsj,isjd->ibd", rounded_probs, value_tiles, preferred_element_type=jnp.float32
    )
    return (attended / row_total[:, :, None]).astype(jnp.bfloat16)


def shards(queries, keys, values, out_weight, vertical, slash):
    local_rows = queries.shape[0]
    local_heads = vertical.shape[0]
    local_blocks = local_rows // BLK
    ctx_rank = lax.axis_index("ctx")
    keyvals = jnp.concatenate([keys, values], axis=1).reshape(local_blocks, BLK, 2 * HS)
    first_block = ctx_rank * local_blocks
    query_blocks = first_block + jnp.arange(local_blocks, dtype=jnp.int32)
    source = lax.all_gather(keyvals, "ctx", axis=0, tiled=True)

    def locate(blocks):
        return jnp.clip(blocks, 0, source.shape[0] - 1)

    head_queries = queries.reshape(local_blocks, BLK, local_heads, HS).transpose(2, 0, 1, 3)

    def one_head(inputs):
        head_query, vert_row, slash_row = inputs
        blocks, usable = slot_table(vert_row, slash_row, query_blocks)
        chosen = source[locate(blocks)]
        return attend(head_query, chosen[..., :HS], chosen[..., HS:], blocks, usable, query_blocks)

    heads_out = lax.map(one_head, (head_queries, vertical, slash))
    attended = heads_out.transpose(1, 2, 0, 3).reshape(local_rows, local_heads * HS)
    product = jnp.dot(attended, out_weight, preferred_element_type=jnp.float32)
    return lax.psum_scatter(
        lax.optimization_barrier(product.astype(jnp.bfloat16))
        .astype(jnp.float32)
        .astype(jnp.bfloat16),
        "tp",
        scatter_dimension=0,
        tiled=True,
    )


def solution(mesh):
    return jax.shard_map(
        shards,
        mesh=mesh,
        in_specs=(
            P("ctx", "tp"),
            P("ctx", "tp"),
            P("ctx", "tp"),
            P("tp", None),
            P("tp", None),
            P("tp", None),
        ),
        out_specs=P(("ctx", "tp"), None),
        check_vma=False,
    )
```

profile of v0, /device:TPU:8, one launch (start us, length us, event | category | flops | bytes accessed | tf_op | source)
XLA Modules:
  0.0 409.9 jit_solution(11067707473191889496)
XLA Ops:
  10.2 105.3 %all-gather.2.cloned.1.call-done = bf16[256,64,256]{2,1,0:T(8,128)(2,1)} async-done(((bf16[8,64,256]{2,1,0:T(8,128)(2,1)}), bf16[256,64,256]{2,1,0:T(8,128)(2,1)}) %all-gather.2.cloned.1.call-update) | async-done | bytes 8388624 | tf_op jit(solution)/shard_map/all_gather | solution.py:56
  115.5 191.7 %while.11 = (s32[]{:T(128)}, bf16[8,8,64,128]{3,2,1,0:T(8,128)(2,1)S(1)}, s32[8,16]{1,0:T(8,128)}, s32[8,8]{1,0:T(8,128)}, bf16[8,8,64,128]{3,2,1,0:T(8,128)(2,1...) while((s32[]{:T(128)}, bf16[8,8,64,128]{3,2,1,0:T(8,128)(2,1)S(1)}, ...), condition=%wide.region_4.5_spmd.clone, body=%wide.region_0.4_spmd.clone.sunk | while | flops 416161856 | bytes 50649856 | solution.py:69
  117.7 11.5 %gather_fusion = bf16[192,64,256]{2,1,0:T(8,128)(2,1)} fusion(bf16[256,64,256]{2,1,0:T(8,128)(2,1)} %get-tuple-element.179, s32[1024]{0:T(1024)S(1)} %pad_clamp_fusion.2), kind=kCustom, calls=%fused_computation.clone.clone.1 | custom fusion | bytes 12583680 | tf_op jit(solution)/shard_map/while/body/eval_jaxpr/gather | solution.py:66
  129.2 4.4 %fusion.61 = (f32[8,64]{1,0:T(8,128)S(1)}, f32[8,64,24,64]{1,3,2,0:T(8,128)S(1)}) fusion(pred[64,64]{0,1:T(8,128)(4,1)S(1)} %iota_compare_fusion.2, pred[8,24]{1,0:T(8,128)(4,1)S(1)} %get-tuple-element.152, pred[8,24]{1,0:T(8,128)(4,1)S(1)} %get-tuple-element.153, bf16[8,24,64,256]{3,2,1,0:T(8,128)(2,1)} %bitcast.59, ...), kind=kOutput, calls=%fused_computation.6.clone.1 | convolution fusion | flops 205258240 | bytes 6435328 | tf_op jit(solution)/shard_map/while/body/eval_jaxpr/ibd,isjd->ibsj/dot_general | solution.py:27
  133.6 2.5 fusion.62
  136.1 3.4 fusion.63
  141.6 11.5 %gather_fusion = bf16[192,64,256]{2,1,0:T(8,128)(2,1)} fusion(bf16[256,64,256]{2,1,0:T(8,128)(2,1)} %get-tuple-element.179, s32[1024]{0:T(1024)S(1)} %pad_clamp_fusion.2), kind=kCustom, calls=%fused_computation.clone.clone.1 | custom fusion | bytes 12583680 | tf_op jit(solution)/shard_map/while/body/eval_jaxpr/gather | solution.py:66
  153.1 4.4 %fusion.61 = (f32[8,64]{1,0:T(8,128)S(1)}, f32[8,64,24,64]{1,3,2,0:T(8,128)S(1)}) fusion(pred[64,64]{0,1:T(8,128)(4,1)S(1)} %iota_compare_fusion.2, pred[8,24]{1,0:T(8,128)(4,1)S(1)} %get-tuple-element.152, pred[8,24]{1,0:T(8,128)(4,1)S(1)} %get-tuple-element.153, bf16[8,24,64,256]{3,2,1,0:T(8,128)(2,1)} %bitcast.59, ...), kind=kOutput, calls=%fused_computation.6.clone.1 | convolution fusion | flops 205258240 | bytes 6435328 | tf_op jit(solution)/shard_map/while/body/eval_jaxpr/ibd,isjd->ibsj/dot_general | solution.py:27
  160.0 3.4 fusion.63
  165.6 11.5 %gather_fusion = bf16[192,64,256]{2,1,0:T(8,128)(2,1)} fusion(bf16[256,64,256]{2,1,0:T(8,128)(2,1)} %get-tuple-element.179, s32[1024]{0:T(1024)S(1)} %pad_clamp_fusion.2), kind=kCustom, calls=%fused_computation.clone.clone.1 | custom fusion | bytes 12583680 | tf_op jit(solution)/shard_map/while/body/eval_jaxpr/gather | solution.py:66
  177.1 4.4 %fusion.61 = (f32[8,64]{1,0:T(8,128)S(1)}, f32[8,64,24,64]{1,3,2,0:T(8,128)S(1)}) fusion(pred[64,64]{0,1:T(8,128)(4,1)S(1)} %iota_compare_fusion.2, pred[8,24]{1,0:T(8,128)(4,1)S(1)} %get-tuple-element.152, pred[8,24]{1,0:T(8,128)(4,1)S(1)} %get-tuple-element.153, bf16[8,24,64,256]{3,2,1,0:T(8,128)(2,1)} %bitcast.59, ...), kind=kOutput, calls=%fused_computation.6.clone.1 | convolution fusion | flops 205258240 | bytes 6435328 | tf_op jit(solution)/shard_map/while/body/eval_jaxpr/ibd,isjd->ibsj/dot_general | solution.py:27
  181.5 2.5 fusion.62
  184.0 3.4 fusion.63
  189.5 11.5 %gather_fusion = bf16[192,64,256]{2,1,0:T(8,128)(2,1)} fusion(bf16[256,64,256]{2,1,0:T(8,128)(2,1)} %get-tuple-element.179, s32[1024]{0:T(1024)S(1)} %pad_clamp_fusion.2), kind=kCustom, calls=%fused_computation.clone.clone.1 | custom fusion | bytes 12583680 | tf_op jit(solution)/shard_map/while/body/eval_jaxpr/gather | solution.py:66
  201.1 4.4 %fusion.61 = (f32[8,64]{1,0:T(8,128)S(1)}, f32[8,64,24,64]{1,3,2,0:T(8,128)S(1)}) fusion(pred[64,64]{0,1:T(8,128)(4,1)S(1)} %iota_compare_fusion.2, pred[8,24]{1,0:T(8,128)(4,1)S(1)} %get-tuple-element.152, pred[8,24]{1,0:T(8,128)(4,1)S(1)} %get-tuple-element.153, bf16[8,24,64,256]{3,2,1,0:T(8,128)(2,1)} %bitcast.59, ...), kind=kOutput, calls=%fused_computation.6.clone.1 | convolution fusion | flops 205258240 | bytes 6435328 | tf_op jit(solution)/shard_map/while/body/eval_jaxpr/ibd,isjd->ibsj/dot_general | solution.py:27
  205.4 2.5 fusion.62
  208.0 3.4 fusion.63
  213.5 11.5 %gather_fusion = bf16[192,64,256]{2,1,0:T(8,128)(2,1)} fusion(bf16[256,64,256]{2,1,0:T(8,128)(2,1)} %get-tuple-element.179, s32[1024]{0:T(1024)S(1)} %pad_clamp_fusion.2), kind=kCustom, calls=%fused_computation.clone.clone.1 | custom fusion | bytes 12583680 | tf_op jit(solution)/shard_map/while/body/eval_jaxpr/gather | solution.py:66
  225.0 4.4 %fusion.61 = (f32[8,64]{1,0:T(8,128)S(1)}, f32[8,64,24,64]{1,3,2,0:T(8,128)S(1)}) fusion(pred[64,64]{0,1:T(8,128)(4,1)S(1)} %iota_compare_fusion.2, pred[8,24]{1,0:T(8,128)(4,1)S(1)} %get-tuple-element.152, pred[8,24]{1,0:T(8,128)(4,1)S(1)} %get-tuple-element.153, bf16[8,24,64,256]{3,2,1,0:T(8,128)(2,1)} %bitcast.59, ...), kind=kOutput, calls=%fused_computation.6.clone.1 | convolution fusion | flops 205258240 | bytes 6435328 | tf_op jit(solution)/shard_map/while/body/eval_jaxpr/ibd,isjd->ibsj/dot_general | solution.py:27
  229.4 2.5 fusion.62
  231.9 3.4 fusion.63
  237.5 11.5 %gather_fusion = bf16[192,64,256]{2,1,0:T(8,128)(2,1)} fusion(bf16[256,64,256]{2,1,0:T(8,128)(2,1)} %get-tuple-element.179, s32[1024]{0:T(1024)S(1)} %pad_clamp_fusion.2), kind=kCustom, calls=%fused_computation.clone.clone.1 | custom fusion | bytes 12583680 | tf_op jit(solution)/shard_map/while/body/eval_jaxpr/gather | solution.py:66
  249.0 4.4 %fusion.61 = (f32[8,64]{1,0:T(8,128)S(1)}, f32[8,64,24,64]{1,3,2,0:T(8,128)S(1)}) fusion(pred[64,64]{0,1:T(8,128)(4,1)S(1)} %iota_compare_fusion.2, pred[8,24]{1,0:T(8,128)(4,1)S(1)} %get-tuple-element.152, pred[8,24]{1,0:T(8,128)(4,1)S(1)} %get-tuple-element.153, bf16[8,24,64,256]{3,2,1,0:T(8,128)(2,1)} %bitcast.59, ...), kind=kOutput, calls=%fused_computation.6.clone.1 | convolution fusion | flops 205258240 | bytes 6435328 | tf_op jit(solution)/shard_map/while/body/eval_jaxpr/ibd,isjd->ibsj/dot_general | solution.py:27
  255.9 3.4 fusion.63
  261.4 11.5 %gather_fusion = bf16[192,64,256]{2,1,0:T(8,128)(2,1)} fusion(bf16[256,64,256]{2,1,0:T(8,128)(2,1)} %get-tuple-element.179, s32[1024]{0:T(1024)S(1)} %pad_clamp_fusion.2), kind=kCustom, calls=%fused_computation.clone.clone.1 | custom fusion | bytes 12583680 | tf_op jit(solution)/shard_map/while/body/eval_jaxpr/gather | solution.py:66
  272.9 4.4 %fusion.61 = (f32[8,64]{1,0:T(8,128)S(1)}, f32[8,64,24,64]{1,3,2,0:T(8,128)S(1)}) fusion(pred[64,64]{0,1:T(8,128)(4,1)S(1)} %iota_compare_fusion.2, pred[8,24]{1,0:T(8,128)(4,1)S(1)} %get-tuple-element.152, pred[8,24]{1,0:T(8,128)(4,1)S(1)} %get-tuple-element.153, bf16[8,24,64,256]{3,2,1,0:T(8,128)(2,1)} %bitcast.59, ...), kind=kOutput, calls=%fused_computation.6.clone.1 | convolution fusion | flops 205258240 | bytes 6435328 | tf_op jit(solution)/shard_map/while/body/eval_jaxpr/ibd,isjd->ibsj/dot_general | solution.py:27
  279.8 3.4 fusion.63
  285.4 11.5 %gather_fusion = bf16[192,64,256]{2,1,0:T(8,128)(2,1)} fusion(bf16[256,64,256]{2,1,0:T(8,128)(2,1)} %get-tuple-element.179, s32[1024]{0:T(1024)S(1)} %pad_clamp_fusion.2), kind=kCustom, calls=%fused_computation.clone.clone.1 | custom fusion | bytes 12583680 | tf_op jit(solution)/shard_map/while/body/eval_jaxpr/gather | solution.py:66
  296.9 4.4 %fusion.61 = (f32[8,64]{1,0:T(8,128)S(1)}, f32[8,64,24,64]{1,3,2,0:T(8,128)S(1)}) fusion(pred[64,64]{0,1:T(8,128)(4,1)S(1)} %iota_compare_fusion.2, pred[8,24]{1,0:T(8,128)(4,1)S(1)} %get-tuple-element.152, pred[8,24]{1,0:T(8,128)(4,1)S(1)} %get-tuple-element.153, bf16[8,24,64,256]{3,2,1,0:T(8,128)(2,1)} %bitcast.59, ...), kind=kOutput, calls=%fused_computation.6.clone.1 | convolution fusion | flops 205258240 | bytes 6435328 | tf_op jit(solution)/shard_map/while/body/eval_jaxpr/ibd,isjd->ibsj/dot_general | solution.py:27
  303.8 3.4 fusion.63
  307.9 16.8 %convolution_convert_fusion = bf16[512,8192]{1,0:T(8,128)(2,1)} fusion(bf16[1024,8192]{1,0:T(8,128)(2,1)} %param.11, bf16[64,8,8,128]{3,2,1,0:T(8,128)(2,1)S(1)} %bitcast.66), kind=kOutput, calls=%fused_computation.42 | convolution fusion | flops 8594128896 | bytes 26214400 | tf_op jit(solution)/shard_map/dot_general | solution.py:71
  324.7 78.3 %reduce-scatter.2.cloned.1.call-done = bf16[128,8192]{1,0:T(8,128)(2,1)} async-done(((bf16[512,8192]{1,0:T(8,128)(2,1)}), bf16[128,8192]{1,0:T(8,128)(2,1)}) %reduce-scatter.2.cloned.1.call-update) | async-done | bytes 2097168 | tf_op jit(solution)/shard_map/reduce_scatter | solution.py:72
  (166 shorter events, 31.6 us)
Async XLA Ops:
  6.5 109.0 %all-gather.2.cloned.1.call-start = ((), (), s32[]{:S(2)}) async-start(), calls=%async_computation.1 | async-start | bytes 8650752 | tf_op jit(solution)/shard_map/all_gather | solution.py:56
  8.3 394.8 %reduce-scatter.2.cloned.1.call-start = ((), (), s32[]{:S(2)}) async-start(), calls=%async_computation.2 | async-start | bytes 10485760 | tf_op jit(solution)/shard_map/reduce_scatter | solution.py:72
  129.2 6.9 %slice-start = ((s8[6291456]{0:T(1024)(128)(4,1)}), s8[4194304]{0:T(1024)(128)(4,1)S(1)}, s32[]{:S(2)}) async-start(s8[6291456]{0:T(1024)(128)(4,1)} %bitcast.60), calls=%async_computation.3 | async-start | bytes 8388608 | tf_op jit(solution)/shard_map/while
  129.2 6.9 %slice-start.1 = ((s8[6291456]{0:T(1024)(128)(4,1)}), s8[2097152]{0:T(1024)(128)(4,1)S(1)}, s32[]{:S(2)}) async-start(s8[6291456]{0:T(1024)(128)(4,1)} %bitcast.60), calls=%async_computation.4 | async-start | bytes 4194304 | tf_op jit(solution)/shard_map/while
  153.1 6.9 %slice-start = ((s8[6291456]{0:T(1024)(128)(4,1)}), s8[4194304]{0:T(1024)(128)(4,1)S(1)}, s32[]{:S(2)}) async-start(s8[6291456]{0:T(1024)(128)(4,1)} %bitcast.60), calls=%async_computation.3 | async-start | bytes 8388608 | tf_op jit(solution)/shard_map/while
  153.1 6.9 %slice-start.1 = ((s8[6291456]{0:T(1024)(128)(4,1)}), s8[2097152]{0:T(1024)(128)(4,1)S(1)}, s32[]{:S(2)}) async-start(s8[6291456]{0:T(1024)(128)(4,1)} %bitcast.60), calls=%async_computation.4 | async-start | bytes 4194304 | tf_op jit(solution)/shard_map/while
  177.1 6.9 %slice-start = ((s8[6291456]{0:T(1024)(128)(4,1)}), s8[4194304]{0:T(1024)(128)(4,1)S(1)}, s32[]{:S(2)}) async-start(s8[6291456]{0:T(1024)(128)(4,1)} %bitcast.60), calls=%async_computation.3 | async-start | bytes 8388608 | tf_op jit(solution)/shard_map/while
  177.1 6.9 %slice-start.1 = ((s8[6291456]{0:T(1024)(128)(4,1)}), s8[2097152]{0:T(1024)(128)(4,1)S(1)}, s32[]{:S(2)}) async-start(s8[6291456]{0:T(1024)(128)(4,1)} %bitcast.60), calls=%async_computation.4 | async-start | bytes 4194304 | tf_op jit(solution)/shard_map/while
  201.0 6.9 %slice-start = ((s8[6291456]{0:T(1024)(128)(4,1)}), s8[4194304]{0:T(1024)(128)(4,1)S(1)}, s32[]{:S(2)}) async-start(s8[6291456]{0:T(1024)(128)(4,1)} %bitcast.60), calls=%async_computation.3 | async-start | bytes 8388608 | tf_op jit(solution)/shard_map/while
  201.0 6.9 %slice-start.1 = ((s8[6291456]{0:T(1024)(128)(4,1)}), s8[2097152]{0:T(1024)(128)(4,1)S(1)}, s32[]{:S(2)}) async-start(s8[6291456]{0:T(1024)(128)(4,1)} %bitcast.60), calls=%async_computation.4 | async-start | bytes 4194304 | tf_op jit(solution)/shard_map/while
  225.0 6.9 %slice-start = ((s8[6291456]{0:T(1024)(128)(4,1)}), s8[4194304]{0:T(1024)(128)(4,1)S(1)}, s32[]{:S(2)}) async-start(s8[6291456]{0:T(1024)(128)(4,1)} %bitcast.60), calls=%async_computation.3 | async-start | bytes 8388608 | tf_op jit(solution)/shard_map/while
  225.0 6.9 %slice-start.1 = ((s8[6291456]{0:T(1024)(128)(4,1)}), s8[2097152]{0:T(1024)(128)(4,1)S(1)}, s32[]{:S(2)}) async-start(s8[6291456]{0:T(1024)(128)(4,1)} %bitcast.60), calls=%async_computation.4 | async-start | bytes 4194304 | tf_op jit(solution)/shard_map/while
  249.0 6.9 %slice-start = ((s8[6291456]{0:T(1024)(128)(4,1)}), s8[4194304]{0:T(1024)(128)(4,1)S(1)}, s32[]{:S(2)}) async-start(s8[6291456]{0:T(1024)(128)(4,1)} %bitcast.60), calls=%async_computation.3 | async-start | bytes 8388608 | tf_op jit(solution)/shard_map/while
  249.0 6.9 %slice-start.1 = ((s8[6291456]{0:T(1024)(128)(4,1)}), s8[2097152]{0:T(1024)(128)(4,1)S(1)}, s32[]{:S(2)}) async-start(s8[6291456]{0:T(1024)(128)(4,1)} %bitcast.60), calls=%async_computation.4 | async-start | bytes 4194304 | tf_op jit(solution)/shard_map/while
  272.9 6.9 %slice-start = ((s8[6291456]{0:T(1024)(128)(4,1)}), s8[4194304]{0:T(1024)(128)(4,1)S(1)}, s32[]{:S(2)}) async-start(s8[6291456]{0:T(1024)(128)(4,1)} %bitcast.60), calls=%async_computation.3 | async-start | bytes 8388608 | tf_op jit(solution)/shard_map/while
  272.9 6.9 %slice-start.1 = ((s8[6291456]{0:T(1024)(128)(4,1)}), s8[2097152]{0:T(1024)(128)(4,1)S(1)}, s32[]{:S(2)}) async-start(s8[6291456]{0:T(1024)(128)(4,1)} %bitcast.60), calls=%async_computation.4 | async-start | bytes 4194304 | tf_op jit(solution)/shard_map/while
  296.9 6.9 %slice-start = ((s8[6291456]{0:T(1024)(128)(4,1)}), s8[4194304]{0:T(1024)(128)(4,1)S(1)}, s32[]{:S(2)}) async-start(s8[6291456]{0:T(1024)(128)(4,1)} %bitcast.60), calls=%async_computation.3 | async-start | bytes 8388608 | tf_op jit(solution)/shard_map/while
  296.9 6.9 %slice-start.1 = ((s8[6291456]{0:T(1024)(128)(4,1)}), s8[2097152]{0:T(1024)(128)(4,1)S(1)}, s32[]{:S(2)}) async-start(s8[6291456]{0:T(1024)(128)(4,1)} %bitcast.60), calls=%async_computation.4 | async-start | bytes 4194304 | tf_op jit(solution)/shard_map/while
Sparse Core Ops, SparseCore 0:
  10.5 104.9 all-gather.1
  324.8 78.1 reduce-scatter.1
where the time goes:
time: 412 us; the launch traced here: 410 us
  waiting for transfers between devices  184 us (45%)
  local copies, waits for them, and re-layouts  106 us (26%)
  matrix products  78.7 us (19%)
  other arithmetic  27 us (7%)
  between operations  13.5 us (3%)
    all_gather x1, waiting for transfers between devices, shards(): source = lax.all_gather(keyvals, 'ctx', axis=0, tiled=True)  105 us
    gather x8, local copies, waits for them, and re-layouts, one_head(): chosen = source[locate(blocks)]  91.9 us
    reduce_scatter x1, waiting for transfers between devices, shards(): lax.psum_scatter(lax.optimization_barrier(product.astype(jnp.bfloat16)).a...  78.3 us
    dot_general x8, matrix products, attend(): jnp.einsum('ibd,isjd->ibsj', head_query, key_tiles, preferred_element_typ...  35.1 us
    dot_general x8, matrix products, attend(): jnp.einsum('ibsj,isjd->ibd', rounded_probs, value_tiles, preferred_elemen...  26.8 us
    reduce_sum x8, other arithmetic, attend(): row_total = jnp.sum(weights, axis=(2, 3))  19.8 us
    dot_general x1, matrix products, shards(): product = jnp.dot(attended, out_weight, preferred_element_type=jnp.float32)  16.8 us
  transfers between devices with their start and end apart: 2, of which 2 were waited for; matrix products, arithmetic and copies ran while one was open for 0% of the time, Pallas kernels for 0%

commit v1 on v0

v1 whole, which is shorter than its diff:
```python
import functools

import jax
import jax.numpy as jnp
from jax import lax
from jax.experimental import pallas as pl
from jax.experimental.pallas import tpu as pltpu
from jax.sharding import PartitionSpec as P

HS = 128
BLK = 64
NEG = -1e30


def attend_kernel(slots, slash, q_ref, kp_ref, vp_ref, kw_ref, vw_ref, bv_ref, bs_ref, o_ref):
    h = pl.program_id(0)
    local_blocks = q_ref.shape[0] // BLK
    nv, ns = slots.shape[1], slash.shape[1]
    reach = kw_ref.shape[0] // BLK - local_blocks
    scale = 1.0 / (HS**0.5)
    k_vert = jnp.concatenate(
        [kp_ref[pl.ds(pl.multiple_of(slots[h, j] * BLK, BLK), BLK), :] for j in range(nv)], axis=0
    )
    v_vert = jnp.concatenate(
        [vp_ref[pl.ds(pl.multiple_of(slots[h, j] * BLK, BLK), BLK), :] for j in range(nv)], axis=0
    )
    row = lax.broadcasted_iota(jnp.int32, (BLK, BLK), 0)
    col = lax.broadcasted_iota(jnp.int32, (BLK, BLK), 1)
    triangle = jnp.where(col > row, NEG, 0.0).astype(jnp.float32)
    triangle = jnp.concatenate([triangle, jnp.zeros((BLK, (ns - 1) * BLK), jnp.float32)], axis=1)
    for pair in range(local_blocks // 2):
        q = q_ref[pl.ds(pair * 2 * BLK, 2 * BLK), :]
        s_vert = lax.dot_general(
            q, k_vert, (((1,), (1,)), ((), ())), preferred_element_type=jnp.float32
        )
        probs, outs, totals = [], [], []
        for half in range(2):
            i = 2 * pair + half
            at = [pl.multiple_of((reach + i - slash[h, j]) * BLK, BLK) for j in range(ns)]
            k_s = jnp.concatenate([kw_ref[pl.ds(a, BLK), :] for a in at], axis=0)
            v_s = jnp.concatenate([vw_ref[pl.ds(a, BLK), :] for a in at], axis=0)
            qi = q[half * BLK : (half + 1) * BLK]
            s_s = lax.dot_general(
                qi, k_s, (((1,), (1,)), ((), ())), preferred_element_type=jnp.float32
            )
            s_s = s_s * scale + (bs_ref[0, pl.ds(i, 1), :] + triangle)
            s_v = s_vert[half * BLK : (half + 1) * BLK] * scale + bv_ref[0, pl.ds(i, 1), :]
            m = jnp.maximum(
                jnp.max(s_v, axis=1, keepdims=True), jnp.max(s_s, axis=1, keepdims=True)
            )
            w_v = jnp.exp(s_v - m)
            w_s = jnp.exp(s_s - m)
            totals.append(
                jnp.sum(w_v, axis=1, keepdims=True) + jnp.sum(w_s, axis=1, keepdims=True)
            )
            probs.append(w_v.astype(jnp.bfloat16))
            outs.append(
                jnp.dot(w_s.astype(jnp.bfloat16), v_s, preferred_element_type=jnp.float32)
            )
        o_v = jnp.dot(
            jnp.concatenate(probs, axis=0), v_vert, preferred_element_type=jnp.float32
        )
        o = (o_v + jnp.concatenate(outs, axis=0)) / jnp.concatenate(totals, axis=0)
        o_ref[pl.ds(pair * 2 * BLK, 2 * BLK), :] = o.astype(jnp.bfloat16)


def shards(ctx_size, queries, keys, values, out_weight, vertical, slash):
    rows, width = queries.shape
    heads, nv = vertical.shape
    ns = slash.shape[1]
    blocks = rows // BLK
    me = lax.axis_index("ctx")
    first = me * blocks

    flat = vertical.reshape(-1)
    mine = flat // blocks == me
    inside = flat % blocks
    low = jnp.min(jnp.where(mine, inside, blocks - 1))
    high = jnp.max(jnp.where(mine, inside, 0))
    kv = jnp.concatenate([keys, values], axis=1)
    picked = jnp.concatenate(
        [
            lax.dynamic_slice_in_dim(kv, low * BLK, BLK, 0),
            lax.dynamic_slice_in_dim(kv, high * BLK, BLK, 0),
        ],
        axis=0,
    )
    pool = lax.all_gather(picked, "ctx", axis=0, tiled=True)
    back1 = lax.ppermute(kv, "ctx", [(i, i + 1) for i in range(ctx_size - 1)])
    back2 = lax.ppermute(kv, "ctx", [(i, i + 2) for i in range(ctx_size - 2)])
    window = jnp.concatenate([back2, back1, kv], axis=0)

    second = jnp.any(
        (flat[:, None] // blocks == flat[None, :] // blocks) & (flat[None, :] < flat[:, None]),
        axis=1,
    )
    slots = (2 * (flat // blocks) + second.astype(jnp.int32)).reshape(heads, nv)
    query_blocks = first + jnp.arange(blocks, dtype=jnp.int32)
    away = query_blocks[None, :, None] - vertical[:, None, :]
    repeated = jnp.any(away[..., None] == slash[:, None, None, :], axis=-1)
    bias_v = jnp.where((away > 0) & ~repeated, 0.0, NEG).astype(jnp.float32)
    bias_s = jnp.where(query_blocks[None, :, None] >= slash[:, None, :], 0.0, NEG)
    bias_v = jnp.broadcast_to(bias_v[..., None], (heads, blocks, nv, BLK)).reshape(
        heads, blocks, nv * BLK
    )
    bias_s = jnp.broadcast_to(
        bias_s.astype(jnp.float32)[..., None], (heads, blocks, ns, BLK)
    ).reshape(heads, blocks, ns * BLK)

    whole = lambda n: pl.BlockSpec((n, HS), lambda h, *_: (0, 0))
    attended = pl.pallas_call(
        attend_kernel,
        out_shape=jax.ShapeDtypeStruct((rows, width), jnp.bfloat16),
        grid_spec=pltpu.PrefetchScalarGridSpec(
            num_scalar_prefetch=2,
            grid=(heads,),
            in_specs=[
                pl.BlockSpec((rows, HS), lambda h, *_: (0, h)),
                pl.BlockSpec((pool.shape[0], HS), lambda h, *_: (0, 0)),
                pl.BlockSpec((pool.shape[0], HS), lambda h, *_: (0, 1)),
                pl.BlockSpec((window.shape[0], HS), lambda h, *_: (0, 0)),
                pl.BlockSpec((window.shape[0], HS), lambda h, *_: (0, 1)),
                pl.BlockSpec((1, blocks, nv * BLK), lambda h, *_: (h, 0, 0)),
                pl.BlockSpec((1, blocks, ns * BLK), lambda h, *_: (h, 0, 0)),
            ],
            out_specs=pl.BlockSpec((rows, HS), lambda h, *_: (0, h)),
        ),
        compiler_params=pltpu.CompilerParams(vmem_limit_bytes=48 << 20),
    )(slots, slash, queries, pool, pool, window, window, bias_v, bias_s)
    product = jnp.dot(attended, out_weight, preferred_element_type=jnp.float32)
    return lax.psum_scatter(
        product.astype(jnp.bfloat16), "tp", scatter_dimension=0, tiled=True
    )


def solution(mesh):
    return jax.shard_map(
        functools.partial(shards, mesh.shape["ctx"]),
        mesh=mesh,
        in_specs=(
            P("ctx", "tp"),
            P("ctx", "tp"),
            P("ctx", "tp"),
            P("tp", None),
            P("tp", None),
            P("tp", None),
        ),
        out_specs=P(("ctx", "tp"), None),
        check_vma=False,
    )
```

time: 412 us -> 220 us (0.53)
  local copies, waits for them, and re-layouts: 106 us -> 6.83 us
  matrix products: 78.7 us -> 16.9 us
  waiting for transfers between devices: 184 us -> 141 us
  Pallas kernels: 0 us -> 24.4 us
  other arithmetic: 27 us -> 5.46 us
  starting transfers between devices: 0.04 us -> 8.85 us
    gather x8 -> x0, local copies, waits for them, and re-layouts: 91.9 us -> none  [one_head(): chosen = source[locate(blocks)]]
    dot_general x16 -> x0, matrix products: 61.9 us -> none  [the longest x8 35.1 us: attend(): jnp.einsum('ibd,isjd->ibsj', head_query, key_tiles, preferred_element_typ...]
    all_gather x1, waiting for transfers between devices: 105 us -> 60.7 us  [shards(): pool = lax.all_gather(picked, 'ctx', axis=0, tiled=True)]
    pallas_call x0 -> x1, Pallas kernels: none -> 24.4 us  [shards(): pl.pallas_call(attend_kernel, out_shape=jax.ShapeDtypeStruct((rows, width...]
    reduce_sum x8 -> x0, other arithmetic: 19.8 us -> none  [attend(): row_total = jnp.sum(weights, axis=(2, 3))]
    ppermute x0 -> x2, starting transfers between devices: none -> 8.81 us  [the longest x1 5.32 us: shards(): back2 = lax.ppermute(kv, 'ctx', [(i, i + 2) for i in range(ctx_size - 2)])]
    sub x8 -> x0, local copies, waits for them, and re-layouts: 5.56 us -> none  [slot_table(): slash_blocks = column_ids - slash_row[None, :]]
    broadcast_in_dim x16 -> x2, local copies, waits for them, and re-layouts: 5.54 us -> 0.31 us  [the longest x1 0.19 us: shards(): jnp.broadcast_to(bias_v[..., None], (heads, blocks, nv, BLK))]
  transfers between devices with their start and end apart: 2 -> 4, of which waited for: 2 -> 3; matrix products, arithmetic and copies ran while one was open for 0% -> 2% of each run, Pallas kernels for 0% -> 0%
where the time goes in v1:
time: 220 us; the launch traced here: 218 us
  waiting for transfers between devices  141 us (64%)
  Pallas kernels  24.4 us (11%)
  matrix products  16.9 us (8%)
  between operations  14.9 us (7%)
  starting transfers between devices  8.85 us (4%)
  local copies, waits for them, and re-layouts  6.83 us (3%)
  other arithmetic  5.46 us (2%)
    reduce_scatter x1, waiting for transfers between devices, shards(): lax.psum_scatter(product.astype(jnp.bfloat16), 'tp', scatter_dimension=0,...  78.2 us
    all_gather x1, waiting for transfers between devices, shards(): pool = lax.all_gather(picked, 'ctx', axis=0, tiled=True)  60.7 us
    pallas_call x1, Pallas kernels, shards(): pl.pallas_call(attend_kernel, out_shape=jax.ShapeDtypeStruct((rows, width...  24.4 us
    dot_general x1, matrix products, shards(): product = jnp.dot(attended, out_weight, preferred_element_type=jnp.float32)  16.9 us
    ppermute x1, starting transfers between devices, shards(): back2 = lax.ppermute(kv, 'ctx', [(i, i + 2) for i in range(ctx_size - 2)])  5.32 us
    unnamed x7, local copies, waits for them, and re-layouts  4.43 us
  transfers between devices with their start and end apart: 4, of which 3 were waited for; matrix products, arithmetic and copies ran while one was open for 2% of the time, Pallas kernels for 0%

profile of v1, /device:TPU:8, one launch (start us, length us, event | category | flops | bytes accessed | tf_op | source)
XLA Modules:
  0.0 217.8 jit_solution(1968428852556623720)
XLA Ops:
  6.5 0.0 all-gather.2.cloned.1.call-start
  6.5 0.8 broadcast_in_dim_reshape.2
  7.3 0.2 and_reduce_fusion
  7.5 0.1 reshape.149
  7.6 1.4 select_reduce_fusion.1
  10.4 0.9 constant_dynamic-update-slice_fusion.1
  11.3 0.9 constant_dynamic-update-slice_fusion
  12.3 0.6 pad_maximum_fusion.1
  12.9 0.0 all-gather.2.cloned.1.call-update
  12.9 0.0 reduce-scatter.2.cloned.1.call-start
  13.0 3.5 %collective-permute-start.1 = (bf16[512,256]{1,0:T(8,128)(2,1)S(1)}, bf16[512,256]{1,0:T(8,128)(2,1)S(1)}, u32[]{:S(2)}, u32[]{:S(2)}) collective-permute-start(bf16[512,256]{1,0:T(8,128)(2,1)S(1)} %constant_dynamic-update-slice_fusion), channel_id=1, source_target_pairs={{0,4},{4,8},{8,12},{12,16},{16,20},{20,24},{24,28},{28,32},{32,36}... | collective-permute-start | bytes 786440 | tf_op jit(solution)/shard_map/ppermute | solution.py:89
  16.5 5.3 %collective-permute-start = (bf16[512,256]{1,0:T(8,128)(2,1)S(1)}, bf16[512,256]{1,0:T(8,128)(2,1)S(1)}, u32[]{:S(2)}, u32[]{:S(2)}) collective-permute-start(bf16[512,256]{1,0:T(8,128)(2,1)S(1)} %constant_dynamic-update-slice_fusion), channel_id=1, source_target_pairs={{0,8},{4,12},{8,16},{12,20},{16,24},{20,28},{24,32},{28,36},{32,40... | collective-permute-start | bytes 786440 | tf_op jit(solution)/shard_map/ppermute | solution.py:90
  21.8 0.8 broadcast_subtract_fusion
  22.6 0.8 compare_select_fusion
  23.3 0.8 compare_reduce_fusion
  24.2 0.1 broadcast_in_dim.42
  24.3 0.1 reshape.148.bs_ref
  24.4 0.8 and_select_fusion
  25.2 0.2 broadcast_in_dim.39
  25.4 0.2 reshape.147.bv_ref
  25.6 0.0 collective-permute-done.1
  25.6 1.6 collective-permute-done
  27.2 0.1 pad_maximum_fusion.kw_ref.vw_ref
  27.2 60.7 %all-gather.2.cloned.1.call-done.kp_ref.vp_ref = bf16[4096,256]{1,0:T(8,128)(2,1)} async-done(((bf16[128,256]{1,0:T(8,128)(2,1)}), bf16[4096,256]{1,0:T(8,128)(2,1)}) %all-gather.2.cloned.1.call-update) | async-done | bytes 2097168 | tf_op jit(solution)/shard_map/all_gather | solution.py:88
  87.9 0.0 copy-start
  87.9 1.6 copy-done
  89.5 1.2 copy-done.1
  90.8 0.7 copy-done.2
  91.4 24.4 %shard_map.64 = bf16[512,1024]{1,0:T(8,128)(2,1)S(1)} custom-call(s32[8,16]{1,0:T(8,128)S(1)} %get-tuple-element.9.slots, s32[8,8]{1,0:T(8,128)S(1)} %copy-done.2, bf16[512,1024]{1,0:T(8,128)(2,1)S(1)} %copy-done.1, bf16[4096,256]{1,0:T(8,128)(2,1)S(1)} %copy-done, bf16[4096,256]{1,0:T(8,128)(2,1)S(1)} %copy-done, ...), custom_call_target="tpu_custom_call" | custom-call | tf_op jit(solution)/shard_map/pallas_call | solution.py:111
  115.9 16.9 %convolution_convert_fusion = bf16[512,8192]{1,0:T(8,128)(2,1)} fusion(bf16[512,1024]{1,0:T(8,128)(2,1)S(1)} %shard_map.64, bf16[1024,8192]{1,0:T(8,128)(2,1)} %param.9), kind=kOutput, calls=%fused_computation | convolution fusion | flops 8594128896 | bytes 26214400 | tf_op jit(solution)/shard_map/dot_general | solution.py:130
  132.7 0.0 reduce-scatter.2.cloned.1.call-update
  132.8 78.2 %reduce-scatter.2.cloned.1.call-done = bf16[128,8192]{1,0:T(8,128)(2,1)} async-done(((bf16[512,8192]{1,0:T(8,128)(2,1)}), bf16[128,8192]{1,0:T(8,128)(2,1)}) %reduce-scatter.2.cloned.1.call-update) | async-done | bytes 2097168 | tf_op jit(solution)/shard_map/reduce_scatter | solution.py:131
  (6 shorter events, 0.0 us)
Async XLA Ops:
  6.5 81.4 %all-gather.2.cloned.1.call-start = ((), (), s32[]{:S(2)}) async-start(), calls=%async_computation.1 | async-start | bytes 2162688 | tf_op jit(solution)/shard_map/all_gather | solution.py:88
  12.9 198.0 %reduce-scatter.2.cloned.1.call-start = ((), (), s32[]{:S(2)}) async-start(), calls=%async_computation.2 | async-start | bytes 10485760 | tf_op jit(solution)/shard_map/reduce_scatter | solution.py:131
  13.0 12.6 %collective-permute-start.1 = (bf16[512,256]{1,0:T(8,128)(2,1)S(1)}, bf16[512,256]{1,0:T(8,128)(2,1)S(1)}, u32[]{:S(2)}, u32[]{:S(2)}) collective-permute-start(bf16[512,256]{1,0:T(8,128)(2,1)S(1)} %constant_dynamic-update-slice_fusion), channel_id=1, source_target_pairs={{0,4},{4,8},{8,12},{12,16},{16,20},{20,24},{24,28},{28,32},{32,36}... | collective-permute-start | bytes 786440 | tf_op jit(solution)/shard_map/ppermute | solution.py:89
  16.5 10.7 %collective-permute-start = (bf16[512,256]{1,0:T(8,128)(2,1)S(1)}, bf16[512,256]{1,0:T(8,128)(2,1)S(1)}, u32[]{:S(2)}, u32[]{:S(2)}) collective-permute-start(bf16[512,256]{1,0:T(8,128)(2,1)S(1)} %constant_dynamic-update-slice_fusion), channel_id=1, source_target_pairs={{0,8},{4,12},{8,16},{12,20},{16,24},{20,28},{24,32},{28,36},{32,40... | collective-permute-start | bytes 786440 | tf_op jit(solution)/shard_map/ppermute | solution.py:90
  87.9 1.6 copy-start
  89.5 1.2 copy-start.1
  90.8 0.7 copy-start.2
Sparse Core Ops, SparseCore 0:
  13.1 74.8 all-gather.1
  132.9 78.0 reduce-scatter.1

commit v2 on v1

v2 whole, which is shorter than its diff:
```python
import functools

import jax
import jax.numpy as jnp
from jax import lax
from jax.experimental import pallas as pl
from jax.experimental.pallas import tpu as pltpu
from jax.sharding import PartitionSpec as P

HS = 128
BLK = 64
NEG = -1e30


MESH = pl.DeviceIdType.MESH
WIDE = 1024


def attend_head(h, base, slots, slash, q_ref, kp_ref, kw_ref, bv_ref, bs_ref, att_ref):
    nv, ns = slots.shape[1], slash.shape[1]
    local_blocks = q_ref.shape[0] // BLK
    reach = kw_ref.shape[0] - local_blocks
    scale = 1.0 / (HS**0.5)
    lanes = pl.ds(pl.multiple_of(h * HS, HS), HS)
    at_v = [slots[h, j] for j in range(nv)]
    k_vert = jnp.concatenate([kp_ref[a, :, :HS] for a in at_v], axis=0)
    v_vert = jnp.concatenate([kp_ref[a, :, HS:] for a in at_v], axis=0)
    row = lax.broadcasted_iota(jnp.int32, (BLK, BLK), 0)
    col = lax.broadcasted_iota(jnp.int32, (BLK, BLK), 1)
    triangle = jnp.where(col > row, NEG, 0.0).astype(jnp.float32)
    triangle = jnp.concatenate([triangle, jnp.zeros((BLK, (ns - 1) * BLK), jnp.float32)], axis=1)
    q = q_ref[pl.ds(pl.multiple_of(base * BLK, BLK), 2 * BLK), lanes]
    s_vert = lax.dot_general(
        q, k_vert, (((1,), (1,)), ((), ())), preferred_element_type=jnp.float32
    )
    probs, outs, totals = [], [], []
    for half in range(2):
        i = base + half
        at = [reach + i - slash[h, j] for j in range(ns)]
        k_s = jnp.concatenate([kw_ref[a, :, :HS] for a in at], axis=0)
        v_s = jnp.concatenate([kw_ref[a, :, HS:] for a in at], axis=0)
        qi = q[half * BLK : (half + 1) * BLK]
        s_s = lax.dot_general(
            qi, k_s, (((1,), (1,)), ((), ())), preferred_element_type=jnp.float32
        )
        s_s = s_s * scale + (bs_ref[h, pl.ds(i, 1), :] + triangle)
        s_v = s_vert[half * BLK : (half + 1) * BLK] * scale + bv_ref[h, pl.ds(i, 1), :]
        m = jnp.maximum(jnp.max(s_v, axis=1, keepdims=True), jnp.max(s_s, axis=1, keepdims=True))
        w_v = jnp.exp(s_v - m)
        w_s = jnp.exp(s_s - m)
        totals.append(jnp.sum(w_v, axis=1, keepdims=True) + jnp.sum(w_s, axis=1, keepdims=True))
        probs.append(w_v.astype(jnp.bfloat16))
        outs.append(jnp.dot(w_s.astype(jnp.bfloat16), v_s, preferred_element_type=jnp.float32))
    o_v = jnp.dot(jnp.concatenate(probs, axis=0), v_vert, preferred_element_type=jnp.float32)
    o = (o_v + jnp.concatenate(outs, axis=0)) / jnp.concatenate(totals, axis=0)
    att_ref[:, lanes] = o.astype(jnp.bfloat16)


def layer_kernel(
    slots, slash, q_ref, kp_ref, kw_ref, bv_ref, bs_ref, w_hbm, out_ref,
    att, w, to_sib, from_sib, to_cross, from_cross,
    w_sem, sib_send, sib_recv, cross_send, cross_recv,
):
    heads = slots.shape[0]
    chunks = w.shape[0]
    quarter = out_ref.shape[0] // BLK
    t = lax.axis_index("tp")
    chip, core = t // 2, t % 2
    sibling = 2 * chip + (1 - core)
    cross = 2 * (1 - chip) + core

    barrier = pltpu.get_barrier_semaphore()
    for other in (sibling, cross):
        pl.semaphore_signal(barrier, inc=1, device_id={"tp": other}, device_id_type=MESH)

    def weights(c):
        at = pl.ds(pl.multiple_of(c * WIDE, WIDE), WIDE)
        return pltpu.make_async_copy(w_hbm.at[:, at], w.at[c], w_sem.at[c])

    def hand(k, c):
        return pltpu.make_async_remote_copy(
            src_ref=to_sib.at[k, c],
            dst_ref=from_sib.at[k, c],
            send_sem=sib_send.at[k, c],
            recv_sem=sib_recv.at[k, c],
            device_id={"tp": sibling},
            device_id_type=MESH,
        )

    def over(c):
        return pltpu.make_async_remote_copy(
            src_ref=to_cross.at[c],
            dst_ref=from_cross.at[c],
            send_sem=cross_send.at[c],
            recv_sem=cross_recv.at[c],
            device_id={"tp": cross},
            device_id_type=MESH,
        )

    @pl.loop(0, chunks)
    def _(c):
        weights(c).start()

    pl.semaphore_wait(barrier, 2)

    @pl.loop(0, 4)
    def _(stage):
        there, swap = 1 - stage // 2, 1 - stage % 2
        owner = 2 * (chip + (1 - 2 * chip) * there) + core + (1 - 2 * core) * swap

        @pl.loop(0, heads)
        def _(h):
            attend_head(h, owner * quarter, slots, slash, q_ref, kp_ref, kw_ref, bv_ref, bs_ref, att)

        @pl.loop(0, chunks)
        def _(c):
            @pl.when(stage == 0)
            def _():
                weights(c).wait()

            y = jnp.dot(att[...], w[c], preferred_element_type=jnp.float32)

            @pl.when(stage == 0)
            def _():
                to_sib[0, c] = y.astype(jnp.bfloat16)
                hand(0, c).start()

            @pl.when(stage == 1)
            def _():
                hand(0, c).wait_recv()
                to_cross[c] = (y + from_sib[0, c].astype(jnp.float32)).astype(jnp.bfloat16)
                over(c).start()

            @pl.when(stage == 2)
            def _():
                to_sib[1, c] = y.astype(jnp.bfloat16)
                hand(1, c).start()

            @pl.when(stage == 3)
            def _():
                hand(1, c).wait_recv()
                over(c).wait_recv()
                at = pl.ds(pl.multiple_of(c * WIDE, WIDE), WIDE)
                out_ref[:, at] = (
                    y + from_sib[1, c].astype(jnp.float32) + from_cross[c].astype(jnp.float32)
                ).astype(jnp.bfloat16)

    @pl.loop(0, chunks)
    def _(c):
        hand(0, c).wait_send()
        hand(1, c).wait_send()
        over(c).wait_send()


def shards(ctx_size, queries, keys, values, out_weight, vertical, slash):
    rows, width = queries.shape
    heads, nv = vertical.shape
    ns = slash.shape[1]
    blocks = rows // BLK
    me = lax.axis_index("ctx")
    first = me * blocks

    flat = vertical.reshape(-1)
    mine = flat // blocks == me
    inside = flat % blocks
    low = jnp.min(jnp.where(mine, inside, blocks - 1))
    high = jnp.max(jnp.where(mine, inside, 0))
    kv = jnp.concatenate([keys, values], axis=1)
    picked = jnp.concatenate(
        [
            lax.dynamic_slice_in_dim(kv, low * BLK, BLK, 0),
            lax.dynamic_slice_in_dim(kv, high * BLK, BLK, 0),
        ],
        axis=0,
    )
    pool = lax.all_gather(picked, "ctx", axis=0, tiled=True)
    back1 = lax.ppermute(kv, "ctx", [(i, i + 1) for i in range(ctx_size - 1)])
    back2 = lax.ppermute(kv, "ctx", [(i, i + 2) for i in range(ctx_size - 2)])
    window = jnp.concatenate([back2, back1, kv], axis=0)

    second = jnp.any(
        (flat[:, None] // blocks == flat[None, :] // blocks) & (flat[None, :] < flat[:, None]),
        axis=1,
    )
    slots = (2 * (flat // blocks) + second.astype(jnp.int32)).reshape(heads, nv)
    query_blocks = first + jnp.arange(blocks, dtype=jnp.int32)
    away = query_blocks[None, :, None] - vertical[:, None, :]
    repeated = jnp.any(away[..., None] == slash[:, None, None, :], axis=-1)
    bias_v = jnp.where((away > 0) & ~repeated, 0.0, NEG).astype(jnp.float32)
    bias_s = jnp.where(query_blocks[None, :, None] >= slash[:, None, :], 0.0, NEG)
    bias_v = jnp.broadcast_to(bias_v[..., None], (heads, blocks, nv, BLK)).reshape(
        heads, blocks, nv * BLK
    )
    bias_s = jnp.broadcast_to(
        bias_s.astype(jnp.float32)[..., None], (heads, blocks, ns, BLK)
    ).reshape(heads, blocks, ns * BLK)

    chunks = out_weight.shape[1] // WIDE
    part = (rows // 4, WIDE)
    vmem = pl.BlockSpec(memory_space=pltpu.VMEM)
    smem = pl.BlockSpec(memory_space=pltpu.SMEM)
    return pl.pallas_call(
        layer_kernel,
        out_shape=jax.ShapeDtypeStruct((rows // 4, out_weight.shape[1]), jnp.bfloat16),
        in_specs=[smem, smem, vmem, vmem, vmem, vmem, vmem, pl.BlockSpec(memory_space=pl.ANY)],
        out_specs=vmem,
        scratch_shapes=[
            pltpu.VMEM((rows // 4, width), jnp.bfloat16),
            pltpu.VMEM((chunks, width, WIDE), jnp.bfloat16),
            pltpu.VMEM((2, chunks) + part, jnp.bfloat16),
            pltpu.VMEM((2, chunks) + part, jnp.bfloat16),
            pltpu.VMEM((chunks,) + part, jnp.bfloat16),
            pltpu.VMEM((chunks,) + part, jnp.bfloat16),
            pltpu.SemaphoreType.DMA((chunks,)),
            pltpu.SemaphoreType.DMA((2, chunks)),
            pltpu.SemaphoreType.DMA((2, chunks)),
            pltpu.SemaphoreType.DMA((chunks,)),
            pltpu.SemaphoreType.DMA((chunks,)),
        ],
        compiler_params=pltpu.CompilerParams(
            collective_id=0, has_side_effects=True, vmem_limit_bytes=52 << 20
        ),
    )(
        slots, slash, queries, pool.reshape(-1, BLK, 2 * HS), window.reshape(-1, BLK, 2 * HS),
        bias_v, bias_s, out_weight,
    )


def solution(mesh):
    return jax.shard_map(
        functools.partial(shards, mesh.shape["ctx"]),
        mesh=mesh,
        in_specs=(
            P("ctx", "tp"),
            P("ctx", "tp"),
            P("ctx", "tp"),
            P("tp", None),
            P("tp", None),
            P("tp", None),
        ),
        out_specs=P(("ctx", "tp"), None),
        check_vma=False,
    )
```

time: 220 us -> 168 us (0.76)
  waiting for transfers between devices: 141 us -> 63 us
  Pallas kernels: 24.4 us -> 68.9 us
  matrix products: 16.9 us -> 0 us
    reduce_scatter x1 -> x0, waiting for transfers between devices: 78.2 us -> none  [shards(): lax.psum_scatter(product.astype(jnp.bfloat16), 'tp', scatter_dimension=0,...]
    pallas_call x1, Pallas kernels: 24.4 us -> 68.9 us  [shards(): pl.pallas_call(layer_kernel, out_shape=jax.ShapeDtypeStruct((rows // 4, o...]
    dot_general x1 -> x0, matrix products: 16.9 us -> none  [shards(): product = jnp.dot(attended, out_weight, preferred_element_type=jnp.float32)]
    unnamed x7 -> x6, local copies, waits for them, and re-layouts: 4.43 us -> 4.04 us
  transfers between devices with their start and end apart: 4 -> 3, of which waited for: 3 -> 2; matrix products, arithmetic and copies ran while one was open for 2% -> 2% of each run, Pallas kernels for 0% -> 0%
where the time goes in v2:
time: 168 us; the launch traced here: 167 us
  Pallas kernels  68.9 us (41%)
  waiting for transfers between devices  63 us (38%)
  between operations  14.8 us (9%)
  starting transfers between devices  8.81 us (5%)
  local copies, waits for them, and re-layouts  6.52 us (4%)
  other arithmetic  4.77 us (3%)
    pallas_call x1, Pallas kernels, shards(): pl.pallas_call(layer_kernel, out_shape=jax.ShapeDtypeStruct((rows // 4, o...  68.9 us
    all_gather x1, waiting for transfers between devices, shards(): pool = lax.all_gather(picked, 'ctx', axis=0, tiled=True)  60.8 us
    ppermute x1, starting transfers between devices, shards(): back2 = lax.ppermute(kv, 'ctx', [(i, i + 2) for i in range(ctx_size - 2)])  5.32 us
    unnamed x6, local copies, waits for them, and re-layouts  4.04 us
    ppermute x1, starting transfers between devices, shards(): back1 = lax.ppermute(kv, 'ctx', [(i, i + 1) for i in range(ctx_size - 1)])  3.48 us
  transfers between devices with their start and end apart: 3, of which 2 were waited for; matrix products, arithmetic and copies ran while one was open for 2% of the time, Pallas kernels for 0%

profile of v2, /device:TPU:8, one launch (start us, length us, event | category | flops | bytes accessed | tf_op | source)
XLA Modules:
  0.0 166.8 jit_solution(1836270090477421353)
XLA Ops:
  6.5 0.0 copy-start.1
  6.5 0.0 all-gather.2.cloned.1.call-start
  6.5 0.8 broadcast_in_dim_reshape.2
  7.4 0.2 and_reduce_fusion
  7.6 0.1 reshape.157
  7.7 1.4 select_reduce_fusion.1
  10.4 0.9 constant_dynamic-update-slice_fusion.1
  11.4 0.9 constant_dynamic-update-slice_fusion
  12.3 0.6 pad_maximum_fusion.1
  13.0 0.0 all-gather.2.cloned.1.call-update
  13.0 3.5 %collective-permute-start.1 = (bf16[512,256]{1,0:T(8,128)(2,1)S(1)}, bf16[512,256]{1,0:T(8,128)(2,1)S(1)}, u32[]{:S(2)}, u32[]{:S(2)}) collective-permute-start(bf16[512,256]{1,0:T(8,128)(2,1)S(1)} %constant_dynamic-update-slice_fusion), channel_id=1, source_target_pairs={{0,4},{4,8},{8,12},{12,16},{16,20},{20,24},{24,28},{28,32},{32,36}... | collective-permute-start | bytes 786440 | tf_op jit(solution)/shard_map/ppermute | solution.py:177
  16.5 5.3 %collective-permute-start = (bf16[512,256]{1,0:T(8,128)(2,1)S(1)}, bf16[512,256]{1,0:T(8,128)(2,1)S(1)}, u32[]{:S(2)}, u32[]{:S(2)}) collective-permute-start(bf16[512,256]{1,0:T(8,128)(2,1)S(1)} %constant_dynamic-update-slice_fusion), channel_id=1, source_target_pairs={{0,8},{4,12},{8,16},{12,20},{16,24},{20,28},{24,32},{28,36},{32,40... | collective-permute-start | bytes 786440 | tf_op jit(solution)/shard_map/ppermute | solution.py:178
  21.8 0.8 broadcast_subtract_fusion
  22.6 0.8 compare_select_fusion
  23.4 0.8 compare_reduce_fusion
  24.2 0.1 broadcast_in_dim.42
  24.3 0.1 reshape.156.bs_ref
  24.5 0.0 copy-done.1
  24.5 0.0 copy-start
  24.5 0.1 and_select_fusion
  24.6 0.2 broadcast_in_dim.39
  24.8 0.2 reshape.155.bv_ref
  24.9 0.0 collective-permute-done.1
  24.9 2.2 %collective-permute-done = bf16[512,256]{1,0:T(8,128)(2,1)S(1)} collective-permute-done((bf16[512,256]{1,0:T(8,128)(2,1)S(1)}, bf16[512,256]{1,0:T(8,128)(2,1)S(1)}, u32[]{:S(2)}, u32[]{:S(2)}) %collective-permute-start) | collective-permute-done | bytes 262176 | tf_op jit(solution)/shard_map/ppermute | solution.py:178
  27.1 0.1 pad_maximum_fusion
  27.2 60.8 %all-gather.2.cloned.1.call-done = bf16[4096,256]{1,0:T(8,128)(2,1)} async-done(((bf16[128,256]{1,0:T(8,128)(2,1)}), bf16[4096,256]{1,0:T(8,128)(2,1)}) %all-gather.2.cloned.1.call-update) | async-done | bytes 2097168 | tf_op jit(solution)/shard_map/all_gather | solution.py:176
  88.0 0.0 copy-done
  88.0 68.9 %shard_map.64 = bf16[128,8192]{1,0:T(8,128)(2,1)} custom-call(s32[8,16]{1,0:T(8,128)S(1)} %get-tuple-element.9.slots, s32[8,8]{1,0:T(8,128)S(1)} %copy-done, bf16[512,1024]{1,0:T(8,128)(2,1)} %q_ref.1, bf16[64,64,256]{2,1,0:T(8,128)(2,1)} %bitcast.7, bf16[24,64,256]{2,1,0:T(8,128)(2,1)S(1)} %bitcast.6, f32[8,8,1024]{2,1,0:T(8,128)S(1)} %reshape.155.bv_ref, ...), custom_call_target="tpu_custom_call" | custom-call | tf_op jit(solution)/shard_map/pallas_call | solution.py:202
  156.9 3.1 %copy.9 = bf16[128,8192]{1,0:T(8,128)(2,1)} copy(bf16[128,8192]{1,0:T(8,128)(2,1)} %shard_map.64) | data formatting | bytes 4194304
  (4 shorter events, 0.0 us)
Async XLA Ops:
  6.5 17.9 %copy-start.1 = (s32[8,16]{1,0:T(8,128)S(1)}, s32[8,16]{1,0:T(8,128)}, u32[]{:S(2)}) copy-start(s32[8,16]{1,0:T(8,128)} %param.10) | copy-start | bytes 1540
  6.5 81.4 %all-gather.2.cloned.1.call-start = ((), (), s32[]{:S(2)}) async-start(), calls=%async_computation | async-start | bytes 2162688 | tf_op jit(solution)/shard_map/all_gather | solution.py:176
  13.0 11.9 %collective-permute-start.1 = (bf16[512,256]{1,0:T(8,128)(2,1)S(1)}, bf16[512,256]{1,0:T(8,128)(2,1)S(1)}, u32[]{:S(2)}, u32[]{:S(2)}) collective-permute-start(bf16[512,256]{1,0:T(8,128)(2,1)S(1)} %constant_dynamic-update-slice_fusion), channel_id=1, source_target_pairs={{0,4},{4,8},{8,12},{12,16},{16,20},{20,24},{24,28},{28,32},{32,36}... | collective-permute-start | bytes 786440 | tf_op jit(solution)/shard_map/ppermute | solution.py:177
  16.5 10.6 %collective-permute-start = (bf16[512,256]{1,0:T(8,128)(2,1)S(1)}, bf16[512,256]{1,0:T(8,128)(2,1)S(1)}, u32[]{:S(2)}, u32[]{:S(2)}) collective-permute-start(bf16[512,256]{1,0:T(8,128)(2,1)S(1)} %constant_dynamic-update-slice_fusion), channel_id=1, source_target_pairs={{0,8},{4,12},{8,16},{12,20},{16,24},{20,28},{24,32},{28,36},{32,40... | collective-permute-start | bytes 786440 | tf_op jit(solution)/shard_map/ppermute | solution.py:178
  24.5 63.5 %copy-start = (s32[8,8]{1,0:T(8,128)S(1)}, s32[8,8]{1,0:T(8,128)}, u32[]{:S(2)}) copy-start(s32[8,8]{1,0:T(8,128)} %slash.1) | copy-start | bytes 772
Sparse Core Ops, SparseCore 0:
  13.1 74.7 all-gather.1

commit v3 on v2

v3 whole, which is shorter than its diff:
```python
import jax
import jax.numpy as jnp
from jax import lax
from jax.experimental import pallas as pl
from jax.experimental.pallas import tpu as pltpu
from jax.sharding import PartitionSpec as P

HS = 128
BLK = 64
NEG = -1e30
MESH = pl.DeviceIdType.MESH
WIDE = 1024
NZ, NX, NY = 4, 2, 4


def attend_head(h, base, slots, vertical, slash, q_ref, pool, window, bv, bs, att):
    nv, ns = vertical.shape[1], slash.shape[1]
    reach = window.shape[0] - q_ref.shape[0] // BLK
    scale = 1.0 / (HS**0.5)
    lanes = pl.ds(pl.multiple_of(h * HS, HS), HS)
    at_v = []
    for j in range(nv):
        s = vertical[h, j] // 8
        at_v.append((s // (NX * NY), (s // NY) % NX, s % NY, slots[h, j]))
    k_vert = jnp.concatenate([pool[a, b, c, d, :, :HS] for a, b, c, d in at_v], axis=0)
    v_vert = jnp.concatenate([pool[a, b, c, d, :, HS:] for a, b, c, d in at_v], axis=0)
    row = lax.broadcasted_iota(jnp.int32, (BLK, BLK), 0)
    col = lax.broadcasted_iota(jnp.int32, (BLK, BLK), 1)
    triangle = jnp.where(col > row, NEG, 0.0).astype(jnp.float32)
    triangle = jnp.concatenate([triangle, jnp.zeros((BLK, (ns - 1) * BLK), jnp.float32)], axis=1)
    q = q_ref[pl.ds(pl.multiple_of(base * BLK, BLK), 2 * BLK), lanes]
    s_vert = lax.dot_general(
        q, k_vert, (((1,), (1,)), ((), ())), preferred_element_type=jnp.float32
    )
    probs, outs, totals = [], [], []
    for half in range(2):
        i = base + half
        at = [reach + i - slash[h, j] for j in range(ns)]
        k_s = jnp.concatenate([window[a, :, :HS] for a in at], axis=0)
        v_s = jnp.concatenate([window[a, :, HS:] for a in at], axis=0)
        qi = q[half * BLK : (half + 1) * BLK]
        s_s = lax.dot_general(
            qi, k_s, (((1,), (1,)), ((), ())), preferred_element_type=jnp.float32
        )
        s_s = s_s * scale + (bs[i, pl.ds(h, 1), :] + triangle)
        s_v = s_vert[half * BLK : (half + 1) * BLK] * scale + bv[i, pl.ds(h, 1), :]
        m = jnp.maximum(jnp.max(s_v, axis=1, keepdims=True), jnp.max(s_s, axis=1, keepdims=True))
        w_v = jnp.exp(s_v - m)
        w_s = jnp.exp(s_s - m)
        totals.append(jnp.sum(w_v, axis=1, keepdims=True) + jnp.sum(w_s, axis=1, keepdims=True))
        probs.append(w_v.astype(jnp.bfloat16))
        outs.append(jnp.dot(w_s.astype(jnp.bfloat16), v_s, preferred_element_type=jnp.float32))
    o_v = jnp.dot(jnp.concatenate(probs, axis=0), v_vert, preferred_element_type=jnp.float32)
    o = (o_v + jnp.concatenate(outs, axis=0)) / jnp.concatenate(totals, axis=0)
    att[:, lanes] = o.astype(jnp.bfloat16)


def spread(values, copies, width):
    lane = lax.broadcasted_iota(jnp.int32, (values.shape[0], copies * width), 1) // width
    out = jnp.zeros(lane.shape, jnp.int32)
    for j in range(copies):
        out = jnp.where(lane == j, values[:, j : j + 1], out)
    return out


def layer_kernel(
    vertical, slash, vert_v, slash_v, q_ref, k_ref, v_ref, w_hbm, out_ref,
    pool, window, bv, bs, slots_v, slots, att, w, to_sib, from_sib, to_cross, from_cross,
    slot_sem, w_sem, sib_send, sib_recv, cross_send, cross_recv, g_send, g_recv,
):
    heads, nv = vertical.shape
    ns = slash.shape[1]
    chunks = w.shape[0]
    quarter = out_ref.shape[0] // BLK
    blocks = k_ref.shape[0]
    reach = window.shape[0] - blocks
    t = lax.axis_index("tp")
    chip, core = t // 2, t % 2
    sibling = 2 * chip + (1 - core)
    cross = 2 * (1 - chip) + core
    me = lax.axis_index("ctx")
    z, x, y = me // (NX * NY), (me // NY) % NX, me % NY
    count = NZ * NX * NY

    def ctx(zz, xx, yy):
        return {"ctx": (zz % NZ) * (NX * NY) + xx * NY + yy % NY}

    after, before = {"ctx": (me + 1) % count}, {"ctx": (me + count - 1) % count}
    barrier = pltpu.get_barrier_semaphore()
    partners = [{"tp": sibling}, {"tp": cross}, after, before, ctx(z, 1 - x, y)]
    partners += [ctx(z, x, y + d) for d in range(1, NY)] + [ctx(z + d, x, y) for d in range(1, NZ)]
    for other in partners:
        pl.semaphore_signal(barrier, inc=1, device_id=other, device_id_type=MESH)

    def weights(c):
        at = pl.ds(pl.multiple_of(c * WIDE, WIDE), WIDE)
        return pltpu.make_async_copy(w_hbm.at[:, at], w.at[c], w_sem.at[c])

    @pl.loop(0, chunks)
    def _(c):
        weights(c).start()

    window[reach:, :, :HS] = k_ref[...]
    window[reach:, :, HS:] = v_ref[...]
    low, high = blocks - 1, 0
    for h in range(heads):
        for j in range(nv):
            v = vertical[h, j]
            mine = v // blocks == me
            low = jnp.minimum(low, jnp.where(mine, v % blocks, blocks - 1))
            high = jnp.maximum(high, jnp.where(mine, v % blocks, 0))
    pool[z, x, y, 0, :, :HS] = k_ref[low]
    pool[z, x, y, 0, :, HS:] = v_ref[low]
    pool[z, x, y, 1, :, :HS] = k_ref[high]
    pool[z, x, y, 1, :, HS:] = v_ref[high]

    pl.semaphore_wait(barrier, len(partners))

    def push(n, ref, to):
        return pltpu.make_async_remote_copy(
            src_ref=ref, dst_ref=ref, send_sem=g_send.at[n], recv_sem=g_recv.at[n],
            device_id=to, device_id_type=MESH,
        )

    def got(n, ref):
        push(n, ref, after).wait_recv()

    sent = []

    def send(n, ref, to):
        copy = push(n, ref, to)
        copy.start()
        sent.append(copy)

    up, down = (z + 1) % NZ, (z + NZ - 1) % NZ
    right, left = (y + 1) % NY, (y + NY - 1) % NY
    send(0, pool.at[z, x, y], ctx(z, 1 - x, y))
    near = pltpu.make_async_remote_copy(
        src_ref=window.at[pl.ds(reach, blocks)], dst_ref=window.at[pl.ds(reach - blocks, blocks)],
        send_sem=g_send.at[15], recv_sem=g_recv.at[15], device_id=after, device_id_type=MESH,
    )
    near.start()

    vert = vert_v[...]
    second = jnp.zeros((heads, nv), jnp.int32)
    for h in range(heads):
        for j in range(nv):
            v = vertical[h, j]
            second = jnp.where((vert // blocks == v // blocks) & (vert > v), 1, second)
    slots_v[...] = second
    place = pltpu.make_async_copy(slots_v, slots, slot_sem)
    place.start()
    vert_wide = spread(vert, nv, BLK)
    slash_wide = spread(slash_v[...], ns, BLK)
    for i in range(blocks):
        block = me * blocks + i
        away = block - vert_wide
        kept = away > 0
        for j in range(ns):
            kept = kept & (away != slash_v[:, j : j + 1])
        bv[i] = jnp.where(kept, 0.0, NEG)
        bs[i] = jnp.where(slash_wide <= block, 0.0, NEG)

    got(0, pool.at[z, 1 - x, y])
    for d in range(1, NY):
        send(d, pool.at[z, :, y, 0], ctx(z, x, y + d))
    for d in range(1, NZ):
        send(3 + d, pool.at[z, :, y, 1], ctx(z + d, x, y))
    for d in range(1, NY):
        got(d, pool.at[z, :, (y + NY - d) % NY, 0])
    send(7, pool.at[z, :, :, 0], ctx(z + 1, x, y))
    send(8, pool.at[z, :, :, 0], ctx(z + NZ - 1, x, y))
    for d in range(1, NZ):
        got(3 + d, pool.at[(z + NZ - d) % NZ, :, y, 1])
    send(9, pool.at[:, :, y, 1], ctx(z, x, y + 1))
    send(10, pool.at[:, :, y, 1], ctx(z, x, y + NY - 1))
    near.wait_recv()
    far = pltpu.make_async_remote_copy(
        src_ref=window.at[pl.ds(reach - blocks + 1, blocks - 1)],
        dst_ref=window.at[pl.ds(reach - 2 * blocks + 1, blocks - 1)],
        send_sem=g_send.at[16], recv_sem=g_recv.at[16], device_id=after, device_id_type=MESH,
    )
    far.start()
    got(7, pool.at[down, :, :, 0])
    send(11, pool.at[down, 0, :, 0], ctx(z + 1, x, y))
    got(8, pool.at[up, :, :, 0])
    send(12, pool.at[up, 1, :, 0], ctx(z + NZ - 1, x, y))
    got(9, pool.at[:, :, left, 1])
    send(13, pool.at[:, 0, left, 1], ctx(z, x, y + 1))
    got(10, pool.at[:, :, right, 1])
    send(14, pool.at[:, 1, right, 1], ctx(z, x, y + NY - 1))
    got(11, pool.at[(z + 2) % NZ, 0, :, 0])
    got(12, pool.at[(z + 2) % NZ, 1, :, 0])
    got(13, pool.at[:, 0, (y + 2) % NY, 1])
    got(14, pool.at[:, 1, (y + 2) % NY, 1])
    far.wait_recv()
    place.wait()

    def hand(k, c):
        return pltpu.make_async_remote_copy(
            src_ref=to_sib.at[k, c],
            dst_ref=from_sib.at[k, c],
            send_sem=sib_send.at[k, c],
            recv_sem=sib_recv.at[k, c],
            device_id={"tp": sibling},
            device_id_type=MESH,
        )

    def over(c):
        return pltpu.make_async_remote_copy(
            src_ref=to_cross.at[c],
            dst_ref=from_cross.at[c],
            send_sem=cross_send.at[c],
            recv_sem=cross_recv.at[c],
            device_id={"tp": cross},
            device_id_type=MESH,
        )

    @pl.loop(0, 4)
    def _(stage):
        there, swap = 1 - stage // 2, 1 - stage % 2
        owner = 2 * (chip + (1 - 2 * chip) * there) + core + (1 - 2 * core) * swap

        @pl.loop(0, heads)
        def _(h):
            attend_head(
                h, owner * quarter, slots, vertical, slash, q_ref, pool, window, bv, bs, att
            )

        @pl.loop(0, chunks)
        def _(c):
            @pl.when(stage == 0)
            def _():
                weights(c).wait()

            part = jnp.dot(att[...], w[c], preferred_element_type=jnp.float32)

            @pl.when(stage == 0)
            def _():
                to_sib[0, c] = part.astype(jnp.bfloat16)
                hand(0, c).start()

            @pl.when(stage == 1)
            def _():
                hand(0, c).wait_recv()
                to_cross[c] = (part + from_sib[0, c].astype(jnp.float32)).astype(jnp.bfloat16)
                over(c).start()

            @pl.when(stage == 2)
            def _():
                to_sib[1, c] = part.astype(jnp.bfloat16)
                hand(1, c).start()

            @pl.when(stage == 3)
            def _():
                hand(1, c).wait_recv()
                over(c).wait_recv()
                at = pl.ds(pl.multiple_of(c * WIDE, WIDE), WIDE)
                out_ref[:, at] = (
                    part + from_sib[1, c].astype(jnp.float32) + from_cross[c].astype(jnp.float32)
                ).astype(jnp.bfloat16)

    @pl.loop(0, chunks)
    def _(c):
        hand(0, c).wait_send()
        hand(1, c).wait_send()
        over(c).wait_send()

    for copy in sent + [near, far]:
        copy.wait_send()


def shards(queries, keys, values, out_weight, vertical, slash):
    rows, width = queries.shape
    heads, nv = vertical.shape
    ns = slash.shape[1]
    blocks = rows // BLK
    chunks = out_weight.shape[1] // WIDE
    part = (rows // 4, WIDE)
    vmem = pl.BlockSpec(memory_space=pltpu.VMEM)
    smem = pl.BlockSpec(memory_space=pltpu.SMEM)
    dma = pltpu.SemaphoreType.DMA
    return pl.pallas_call(
        layer_kernel,
        out_shape=jax.ShapeDtypeStruct((rows // 4, out_weight.shape[1]), jnp.bfloat16),
        in_specs=[smem, smem] + [vmem] * 5 + [pl.BlockSpec(memory_space=pl.ANY)],
        out_specs=vmem,
        scratch_shapes=[
            pltpu.VMEM((NZ, NX, NY, 2, BLK, 2 * HS), jnp.bfloat16),
            pltpu.VMEM((3 * blocks, BLK, 2 * HS), jnp.bfloat16),
            pltpu.VMEM((blocks, heads, nv * BLK), jnp.float32),
            pltpu.VMEM((blocks, heads, ns * BLK), jnp.float32),
            pltpu.VMEM((heads, nv), jnp.int32),
            pltpu.SMEM((heads, nv), jnp.int32),
            pltpu.VMEM((rows // 4, width), jnp.bfloat16),
            pltpu.VMEM((chunks, width, WIDE), jnp.bfloat16),
            pltpu.VMEM((2, chunks) + part, jnp.bfloat16),
            pltpu.VMEM((2, chunks) + part, jnp.bfloat16),
            pltpu.VMEM((chunks,) + part, jnp.bfloat16),
            pltpu.VMEM((chunks,) + part, jnp.bfloat16),
            dma,
            dma((chunks,)),
            dma((2, chunks)),
            dma((2, chunks)),
            dma((chunks,)),
            dma((chunks,)),
            dma((17,)),
            dma((17,)),
        ],
        compiler_params=pltpu.CompilerParams(
            collective_id=0, has_side_effects=True, vmem_limit_bytes=52 << 20
        ),
    )(
        vertical, slash, vertical, slash, queries, keys.reshape(blocks, BLK, HS),
        values.reshape(blocks, BLK, HS), out_weight,
    )


def solution(mesh):
    return jax.shard_map(
        shards,
        mesh=mesh,
        in_specs=(
            P("ctx", "tp"),
            P("ctx", "tp"),
            P("ctx", "tp"),
            P("tp", None),
            P("tp", None),
            P("tp", None),
        ),
        out_specs=P(("ctx", "tp"), None),
        check_vma=False,
    )
```

time: 168 us -> 116 us (0.69)
  waiting for transfers between devices: 63 us -> 0 us
  Pallas kernels: 68.9 us -> 108 us
  between operations: 14.8 us -> 0.01 us
  starting transfers between devices: 8.81 us -> 0 us
  other arithmetic: 4.77 us -> 0 us
    all_gather x1 -> x0, waiting for transfers between devices: 60.8 us -> none  [shards(): pool = lax.all_gather(picked, 'ctx', axis=0, tiled=True)]
    pallas_call x1, Pallas kernels: 68.9 us -> 108 us  [shards(): pl.pallas_call(layer_kernel, out_shape=jax.ShapeDtypeStruct((rows // 4, o...]
    ppermute x2 -> x0, starting transfers between devices: 8.81 us -> none  [the longest x1 5.32 us: shards(): back2 = lax.ppermute(kv, 'ctx', [(i, i + 2) for i in range(ctx_size - 2)])]
    unnamed x6 -> x11, local copies, waits for them, and re-layouts: 4.04 us -> 7.5 us
    ppermute x2 -> x0, waiting for transfers between devices: 2.19 us -> none  [the longest x1 2.19 us: shards(): back2 = lax.ppermute(kv, 'ctx', [(i, i + 2) for i in range(ctx_size - 2)])]
  transfers between devices with their start and end apart: 3 -> 0, of which waited for: 2 -> 0; matrix products, arithmetic and copies ran while one was open for 2% -> 0% of each run, Pallas kernels for 0% -> 0%
where the time goes in v3:
time: 116 us; the launch traced here: 115 us
  Pallas kernels  108 us (93%)
  local copies, waits for them, and re-layouts  7.5 us (6%)
    pallas_call x1, Pallas kernels, shards(): pl.pallas_call(layer_kernel, out_shape=jax.ShapeDtypeStruct((rows // 4, o...  108 us
    unnamed x11, local copies, waits for them, and re-layouts  7.5 us

profile of v3, /device:TPU:8, one launch (start us, length us, event | category | flops | bytes accessed | tf_op | source)
XLA Modules:
  0.0 115.3 jit_solution(11603812222232070202)
XLA Ops:
  0.0 0.0 copy-start
  0.0 1.2 %copy-done = bf16[512,1024]{1,0:T(8,128)(2,1)S(1)} copy-done((bf16[512,1024]{1,0:T(8,128)(2,1)S(1)}, bf16[512,1024]{1,0:T(8,128)(2,1)}, u32[]{:S(2)}) %copy-start) | copy-done | bytes 1048600
  1.2 0.0 copy-start.1
  1.2 0.9 copy-done.1
  2.1 0.0 copy-start.2
  2.1 0.9 copy-done.2
  3.0 0.0 copy-start.3
  3.0 0.7 copy-done.3
  3.7 0.0 copy-start.4
  3.7 0.7 copy-done.4
  4.4 107.8 %shard_map.64 = bf16[128,8192]{1,0:T(8,128)(2,1)} custom-call(s32[8,16]{1,0:T(8,128)S(1)} %copy-done.3, s32[8,8]{1,0:T(8,128)S(1)} %copy-done.4, s32[8,16]{1,0:T(8,128)S(1)} %copy-done.3, s32[8,8]{1,0:T(8,128)S(1)} %copy-done.4, bf16[512,1024]{1,0:T(8,128)(2,1)S(1)} %copy-done, bf16[8,64,128]{2,1,0:T(8,128)(2,1)S(1)} %bitcast.2, ...), custom_call_target="tpu_custom_call" | custom-call | tf_op jit(solution)/shard_map/pallas_call | solution.py:283
  112.2 3.1 %copy.8 = bf16[128,8192]{1,0:T(8,128)(2,1)} copy(bf16[128,8192]{1,0:T(8,128)(2,1)} %shard_map.64) | data formatting | bytes 4194304
Async XLA Ops:
  0.0 1.2 %copy-start = (bf16[512,1024]{1,0:T(8,128)(2,1)S(1)}, bf16[512,1024]{1,0:T(8,128)(2,1)}, u32[]{:S(2)}) copy-start(bf16[512,1024]{1,0:T(8,128)(2,1)} %q_ref.1) | copy-start | bytes 3145732
  1.2 0.9 copy-start.1
  2.1 0.9 copy-start.2
  3.0 0.7 copy-start.3
  3.7 0.7 copy-start.4

commit v4 on v3

--- a/solution.py
+++ b/solution.py
@@ -11,11 +11,12 @@
 MESH = pl.DeviceIdType.MESH
 WIDE = 1024
 NZ, NX, NY = 4, 2, 4
-
-
-def attend_head(h, base, slots, vertical, slash, q_ref, pool, window, bv, bs, att):
+PAIR = 2
+
+
+def attend_head(h, places, slots, vertical, slash, queries, pool, window, bv, bs, out):
     nv, ns = vertical.shape[1], slash.shape[1]
-    reach = window.shape[0] - q_ref.shape[0] // BLK
+    reach = window.shape[0] - queries.shape[0]
     scale = 1.0 / (HS**0.5)
     lanes = pl.ds(pl.multiple_of(h * HS, HS), HS)
     at_v = []
@@ -28,13 +29,12 @@
     col = lax.broadcasted_iota(jnp.int32, (BLK, BLK), 1)
     triangle = jnp.where(col > row, NEG, 0.0).astype(jnp.float32)
     triangle = jnp.concatenate([triangle, jnp.zeros((BLK, (ns - 1) * BLK), jnp.float32)], axis=1)
-    q = q_ref[pl.ds(pl.multiple_of(base * BLK, BLK), 2 * BLK), lanes]
+    q = jnp.concatenate([queries[i, :, lanes] for i in places], axis=0)
     s_vert = lax.dot_general(
         q, k_vert, (((1,), (1,)), ((), ())), preferred_element_type=jnp.float32
     )
     probs, outs, totals = [], [], []
-    for half in range(2):
-        i = base + half
+    for half, i in enumerate(places):
         at = [reach + i - slash[h, j] for j in range(ns)]
         k_s = jnp.concatenate([window[a, :, :HS] for a in at], axis=0)
         v_s = jnp.concatenate([window[a, :, HS:] for a in at], axis=0)
@@ -52,7 +52,9 @@
         outs.append(jnp.dot(w_s.astype(jnp.bfloat16), v_s, preferred_element_type=jnp.float32))
     o_v = jnp.dot(jnp.concatenate(probs, axis=0), v_vert, preferred_element_type=jnp.float32)
     o = (o_v + jnp.concatenate(outs, axis=0)) / jnp.concatenate(totals, axis=0)
-    att[:, lanes] = o.astype(jnp.bfloat16)
+    o = o.astype(jnp.bfloat16)
+    out[0, :, lanes] = o[:BLK]
+    out[1, :, lanes] = o[BLK:]
 
 
 def spread(values, copies, width):
@@ -64,20 +66,22 @@
 
 
 def layer_kernel(
-    vertical, slash, vert_v, slash_v, q_ref, k_ref, v_ref, w_hbm, out_ref,
-    pool, window, bv, bs, slots_v, slots, att, w, to_sib, from_sib, to_cross, from_cross,
-    slot_sem, w_sem, sib_send, sib_recv, cross_send, cross_recv, g_send, g_recv,
+    vertical, slash, vert_hbm, slash_hbm, q_hbm, k_hbm, v_hbm, w_hbm, out_ref,
+    k_ref, v_ref, vert_v, slash_v, queries, pool, window, bv, bs, slots_v, slots, att, w,
+    to_sib, from_sib, to_cross, from_cross,
+    in_sem, slot_sem, w_sem, sib_send, sib_recv, cross_send, cross_recv,
+    lend_send, lend_recv, g_send, g_recv,
 ):
     heads, nv = vertical.shape
     ns = slash.shape[1]
     chunks = w.shape[0]
-    quarter = out_ref.shape[0] // BLK
-    blocks = k_ref.shape[0]
+    blocks = k_hbm.shape[0]
     reach = window.shape[0] - blocks
     t = lax.axis_index("tp")
     chip, core = t // 2, t % 2
     sibling = 2 * chip + (1 - core)
     cross = 2 * (1 - chip) + core
+    corner = 2 * (1 - chip) + (1 - core)
     me = lax.axis_index("ctx")
     z, x, y = me // (NX * NY), (me // NY) % NX, me % NY
     count = NZ * NX * NY
@@ -87,7 +91,8 @@
 
     after, before = {"ctx": (me + 1) % count}, {"ctx": (me + count - 1) % count}
     barrier = pltpu.get_barrier_semaphore()
-    partners = [{"tp": sibling}, {"tp": cross}, after, before, ctx(z, 1 - x, y)]
+    mirror = ctx(z, 1 - x, y)
+    partners = [{"tp": sibling}, {"tp": cross}, {**mirror, "tp": cross}, after, before, mirror]
     partners += [ctx(z, x, y + d) for d in range(1, NY)] + [ctx(z + d, x, y) for d in range(1, NZ)]
     for other in partners:
         pl.semaphore_signal(barrier, inc=1, device_id=other, device_id_type=MESH)
@@ -96,12 +101,21 @@
         at = pl.ds(pl.multiple_of(c * WIDE, WIDE), WIDE)
         return pltpu.make_async_copy(w_hbm.at[:, at], w.at[c], w_sem.at[c])
 
+    inputs = [
+        (k_hbm, k_ref),
+        (v_hbm, v_ref),
+        (vert_hbm, vert_v),
+        (slash_hbm, slash_v),
+        (q_hbm, queries),
+    ]
+    inputs = [pltpu.make_async_copy(a, b, in_sem.at[n]) for n, (a, b) in enumerate(inputs)]
+    for copy in inputs:
+        copy.start()
+
     @pl.loop(0, chunks)
     def _(c):
         weights(c).start()
 
-    window[reach:, :, :HS] = k_ref[...]
-    window[reach:, :, HS:] = v_ref[...]
     low, high = blocks - 1, 0
     for h in range(heads):
         for j in range(nv):
@@ -109,10 +123,13 @@
             mine = v // blocks == me
             low = jnp.minimum(low, jnp.where(mine, v % blocks, blocks - 1))
             high = jnp.maximum(high, jnp.where(mine, v % blocks, 0))
-    pool[z, x, y, 0, :, :HS] = k_ref[low]
-    pool[z, x, y, 0, :, HS:] = v_ref[low]
-    pool[z, x, y, 1, :, :HS] = k_ref[high]
-    pool[z, x, y, 1, :, HS:] = v_ref[high]
+    inputs[0].wait()
+    inputs[1].wait()
+    for half, kv in enumerate((k_ref, v_ref)):
+        at = slice(half * HS, (half + 1) * HS)
+        window[reach:, :, at] = kv[...]
+        pool[z, x, y, 0, :, at] = kv[low]
+        pool[z, x, y, 1, :, at] = kv[high]
 
     pl.semaphore_wait(barrier, len(partners))
 
@@ -134,13 +151,15 @@
 
     up, down = (z + 1) % NZ, (z + NZ - 1) % NZ
     right, left = (y + 1) % NY, (y + NY - 1) % NY
-    send(0, pool.at[z, x, y], ctx(z, 1 - x, y))
+    send(0, pool.at[z, x, y], mirror)
     near = pltpu.make_async_remote_copy(
         src_ref=window.at[pl.ds(reach, blocks)], dst_ref=window.at[pl.ds(reach - blocks, blocks)],
         send_sem=g_send.at[15], recv_sem=g_recv.at[15], device_id=after, device_id_type=MESH,
     )
     near.start()
 
+    for copy in inputs[2:]:
+        copy.wait()
     vert = vert_v[...]
     second = jnp.zeros((heads, nv), jnp.int32)
     for h in range(heads):
@@ -206,65 +225,101 @@
             device_id_type=MESH,
         )
 
-    def over(c):
+    def over(half, c):
+        to = {"tp": cross} if half == 0 else {**mirror, "tp": cross}
         return pltpu.make_async_remote_copy(
-            src_ref=to_cross.at[c],
-            dst_ref=from_cross.at[c],
-            send_sem=cross_send.at[c],
-            recv_sem=cross_recv.at[c],
-            device_id={"tp": cross},
+            src_ref=to_cross.at[c, half],
+            dst_ref=from_cross.at[c, half],
+            send_sem=cross_send.at[half, c],
+            recv_sem=cross_recv.at[half, c],
+            device_id=to,
             device_id_type=MESH,
         )
 
-    @pl.loop(0, 4)
-    def _(stage):
-        there, swap = 1 - stage // 2, 1 - stage % 2
-        owner = 2 * (chip + (1 - 2 * chip) * there) + core + (1 - 2 * core) * swap
-
-        @pl.loop(0, heads)
-        def _(h):
-            attend_head(
-                h, owner * quarter, slots, vertical, slash, q_ref, pool, window, bv, bs, att
-            )
-
-        @pl.loop(0, chunks)
-        def _(c):
-            @pl.when(stage == 0)
-            def _():
-                weights(c).wait()
-
-            part = jnp.dot(att[...], w[c], preferred_element_type=jnp.float32)
-
-            @pl.when(stage == 0)
-            def _():
-                to_sib[0, c] = part.astype(jnp.bfloat16)
-                hand(0, c).start()
-
-            @pl.when(stage == 1)
-            def _():
-                hand(0, c).wait_recv()
-                to_cross[c] = (part + from_sib[0, c].astype(jnp.float32)).astype(jnp.bfloat16)
-                over(c).start()
-
-            @pl.when(stage == 2)
-            def _():
-                to_sib[1, c] = part.astype(jnp.bfloat16)
-                hand(1, c).start()
-
-            @pl.when(stage == 3)
-            def _():
-                hand(1, c).wait_recv()
-                over(c).wait_recv()
-                at = pl.ds(pl.multiple_of(c * WIDE, WIDE), WIDE)
-                out_ref[:, at] = (
-                    part + from_sib[1, c].astype(jnp.float32) + from_cross[c].astype(jnp.float32)
-                ).astype(jnp.bfloat16)
+    def lend(n):
+        at = pl.ds(pl.multiple_of(n * PAIR * HS, PAIR * HS), PAIR * HS)
+        return pltpu.make_async_remote_copy(
+            src_ref=att.at[0, :, :, at],
+            dst_ref=att.at[2, :, :, at],
+            send_sem=lend_send.at[n],
+            recv_sem=lend_recv.at[n],
+            device_id=mirror,
+            device_id_type=MESH,
+        )
+
+    def attend(h, places, out):
+        attend_head(h, places, slots, vertical, slash, queries, pool, window, bv, bs, att.at[out])
+
+    def project(first, second, c):
+        rows = jnp.concatenate([att[first], att[second]], axis=0)
+        return jnp.dot(rows, w[c], preferred_element_type=jnp.float32)
+
+    @pl.loop(0, heads)
+    def _(h):
+        attend(h, (2 * corner + 1, 2 * cross + 1), 0)
+
+        @pl.when(h % PAIR == PAIR - 1)
+        def _():
+            lend(h // PAIR).start()
+
+    @pl.loop(0, heads)
+    def _(h):
+        attend(h, (2 * corner, 2 * cross), 1)
+
+    for n in range(heads // PAIR):
+        lend(n).wait_recv()
+
+    @pl.loop(0, chunks)
+    def _(c):
+        weights(c).wait()
+        to_sib[0, c] = project((1, 0), (2, 0), c).astype(jnp.bfloat16)
+        hand(0, c).start()
+
+    @pl.loop(0, chunks)
+    def _(c):
+        part = project((1, 1), (2, 1), c)
+        hand(0, c).wait_recv()
+        part = (part + from_sib[0, c].astype(jnp.float32)).astype(jnp.bfloat16)
+        to_cross[c, 0] = part[:BLK]
+        to_cross[c, 1] = part[BLK:]
+        over(0, c).start()
+        over(1, c).start()
+
+    @pl.loop(0, heads)
+    def _(h):
+        attend(h, (2 * sibling, 2 * sibling + 1), 3)
+
+    @pl.loop(0, chunks)
+    def _(c):
+        to_sib[1, c] = project((3, 0), (3, 1), c).astype(jnp.bfloat16)
+        hand(1, c).start()
+
+    @pl.loop(0, heads)
+    def _(h):
+        attend(h, (2 * t, 2 * t + 1), 4)
+
+    @pl.loop(0, chunks)
+    def _(c):
+        part = project((4, 0), (4, 1), c)
+        hand(1, c).wait_recv()
+        part = part + from_sib[1, c].astype(jnp.float32)
+        at = pl.ds(pl.multiple_of(c * WIDE, WIDE), WIDE)
+        for half in range(2):
+            over(half, c).wait_recv()
+            here = part[half * BLK : (half + 1) * BLK]
+            out_ref[half * BLK : (half + 1) * BLK, at] = (
+                here + from_cross[c, half].astype(jnp.float32)
+            ).astype(jnp.bfloat16)
 
     @pl.loop(0, chunks)
     def _(c):
         hand(0, c).wait_send()
         hand(1, c).wait_send()
-        over(c).wait_send()
+        over(0, c).wait_send()
+        over(1, c).wait_send()
+
+    for n in range(heads // PAIR):
+        lend(n).wait_send()
 
     for copy in sent + [near, far]:
         copy.wait_send()
@@ -283,35 +338,44 @@
     return pl.pallas_call(
         layer_kernel,
         out_shape=jax.ShapeDtypeStruct((rows // 4, out_weight.shape[1]), jnp.bfloat16),
-        in_specs=[smem, smem] + [vmem] * 5 + [pl.BlockSpec(memory_space=pl.ANY)],
+        in_specs=[smem, smem] + [pl.BlockSpec(memory_space=pltpu.HBM)] * 6,
         out_specs=vmem,
         scratch_shapes=[
+            pltpu.VMEM((blocks, BLK, HS), jnp.bfloat16),
+            pltpu.VMEM((blocks, BLK, HS), jnp.bfloat16),
+            pltpu.VMEM((heads, nv), jnp.int32),
+            pltpu.VMEM((heads, ns), jnp.int32),
+            pltpu.VMEM((blocks, BLK, width), jnp.bfloat16),
             pltpu.VMEM((NZ, NX, NY, 2, BLK, 2 * HS), jnp.bfloat16),
             pltpu.VMEM((3 * blocks, BLK, 2 * HS), jnp.bfloat16),
             pltpu.VMEM((blocks, heads, nv * BLK), jnp.float32),
             pltpu.VMEM((blocks, heads, ns * BLK), jnp.float32),
             pltpu.VMEM((heads, nv), jnp.int32),
             pltpu.SMEM((heads, nv), jnp.int32),
-            pltpu.VMEM((rows // 4, width), jnp.bfloat16),
+            pltpu.VMEM((5, 2, BLK, width), jnp.bfloat16),
             pltpu.VMEM((chunks, width, WIDE), jnp.bfloat16),
             pltpu.VMEM((2, chunks) + part, jnp.bfloat16),
             pltpu.VMEM((2, chunks) + part, jnp.bfloat16),
-            pltpu.VMEM((chunks,) + part, jnp.bfloat16),
-            pltpu.VMEM((chunks,) + part, jnp.bfloat16),
+            pltpu.VMEM((chunks, 2, BLK, WIDE), jnp.bfloat16),
+            pltpu.VMEM((chunks, 2, BLK, WIDE), jnp.bfloat16),
+            dma((5,)),
             dma,
             dma((chunks,)),
             dma((2, chunks)),
             dma((2, chunks)),
-            dma((chunks,)),
-            dma((chunks,)),
+            dma((2, chunks)),
+            dma((2, chunks)),
+            dma((heads // PAIR,)),
+            dma((heads // PAIR,)),
             dma((17,)),
             dma((17,)),
         ],
         compiler_params=pltpu.CompilerParams(
-            collective_id=0, has_side_effects=True, vmem_limit_bytes=52 << 20
+            collective_id=0, has_side_effects=True, vmem_limit_bytes=60 << 20
         ),
     )(
-        vertical, slash, vertical, slash, queries, keys.reshape(blocks, BLK, HS),
+        vertical, slash, vertical, slash, queries.reshape(blocks, BLK, width),
+        keys.reshape(blocks, BLK, HS),
         values.reshape(blocks, BLK, HS), out_weight,
     )
 

time: 116 us -> 97.6 us (0.84)
  Pallas kernels: 108 us -> 94.3 us
  local copies, waits for them, and re-layouts: 7.5 us -> 3.1 us
    pallas_call x1, Pallas kernels: 108 us -> 94.3 us  [shards(): pl.pallas_call(layer_kernel, out_shape=jax.ShapeDtypeStruct((rows // 4, o...]
    unnamed x11 -> x1, local copies, waits for them, and re-layouts: 7.5 us -> 3.1 us
where the time goes in v4:
time: 97.6 us; the launch traced here: 97.4 us
  Pallas kernels  94.3 us (97%)
  local copies, waits for them, and re-layouts  3.1 us (3%)
    pallas_call x1, Pallas kernels, shards(): pl.pallas_call(layer_kernel, out_shape=jax.ShapeDtypeStruct((rows // 4, o...  94.3 us
    unnamed x1, local copies, waits for them, and re-layouts  3.1 us

profile of v4, /device:TPU:8, one launch (start us, length us, event | category | flops | bytes accessed | tf_op | source)
XLA Modules:
  0.0 97.4 jit_solution(1234756178562623121)
XLA Ops:
  0.0 94.3 %shard_map.64 = bf16[128,8192]{1,0:T(8,128)(2,1)} custom-call(s32[8,16]{1,0:T(8,128)} %vert_hbm.1, s32[8,8]{1,0:T(8,128)} %slash_hbm.1, s32[8,16]{1,0:T(8,128)} %vert_hbm.1, s32[8,8]{1,0:T(8,128)} %slash_hbm.1, bf16[8,64,1024]{2,1,0:T(8,128)(2,1)} %bitcast.3, bf16[8,64,128]{2,1,0:T(8,128)(2,1)} %bitcast.4, bf16[8,64,128]{2,1,0:T(8,128)(2,1)} %bitcast.5, ...), custom_call_target="tpu_custom_call" | custom-call | tf_op jit(solution)/shard_map/pallas_call | solution.py:338
  94.3 3.1 %copy.8 = bf16[128,8192]{1,0:T(8,128)(2,1)} copy(bf16[128,8192]{1,0:T(8,128)(2,1)} %shard_map.64) | data formatting | bytes 4194304

commit v5 on v4

--- a/solution.py
+++ b/solution.py
@@ -11,50 +11,51 @@
 MESH = pl.DeviceIdType.MESH
 WIDE = 1024
 NZ, NX, NY = 4, 2, 4
-PAIR = 2
-
-
-def attend_head(h, places, slots, vertical, slash, queries, pool, window, bv, bs, out):
-    nv, ns = vertical.shape[1], slash.shape[1]
+TOGETHER = 2
+
+
+def attend_heads(hs, places, slots, slash, queries, pool, window, bv, bs, att, to):
+    nv, ns = slots.shape[1], slash.shape[1]
     reach = window.shape[0] - queries.shape[0]
-    scale = 1.0 / (HS**0.5)
-    lanes = pl.ds(pl.multiple_of(h * HS, HS), HS)
-    at_v = []
-    for j in range(nv):
-        s = vertical[h, j] // 8
-        at_v.append((s // (NX * NY), (s // NY) % NX, s % NY, slots[h, j]))
-    k_vert = jnp.concatenate([pool[a, b, c, d, :, :HS] for a, b, c, d in at_v], axis=0)
-    v_vert = jnp.concatenate([pool[a, b, c, d, :, HS:] for a, b, c, d in at_v], axis=0)
+    scale = 1.4426950408889634 / (HS**0.5)
+    over_keys = (((1,), (1,)), ((), ()))
     row = lax.broadcasted_iota(jnp.int32, (BLK, BLK), 0)
     col = lax.broadcasted_iota(jnp.int32, (BLK, BLK), 1)
     triangle = jnp.where(col > row, NEG, 0.0).astype(jnp.float32)
-    triangle = jnp.concatenate([triangle, jnp.zeros((BLK, (ns - 1) * BLK), jnp.float32)], axis=1)
-    q = jnp.concatenate([queries[i, :, lanes] for i in places], axis=0)
-    s_vert = lax.dot_general(
-        q, k_vert, (((1,), (1,)), ((), ())), preferred_element_type=jnp.float32
-    )
-    probs, outs, totals = [], [], []
-    for half, i in enumerate(places):
-        at = [reach + i - slash[h, j] for j in range(ns)]
-        k_s = jnp.concatenate([window[a, :, :HS] for a in at], axis=0)
-        v_s = jnp.concatenate([window[a, :, HS:] for a in at], axis=0)
-        qi = q[half * BLK : (half + 1) * BLK]
-        s_s = lax.dot_general(
-            qi, k_s, (((1,), (1,)), ((), ())), preferred_element_type=jnp.float32
+    lanes = [pl.ds(pl.multiple_of(h * HS, HS), HS) for h in hs]
+    scores, v_vert, v_slash = [], [], []
+    for h, lane in zip(hs, lanes):
+        at_v = [slots[h, j] for j in range(nv)]
+        k_vert = jnp.concatenate([pool[a, :, :HS] for a in at_v], axis=0)
+        v_vert.append(jnp.concatenate([pool[a, :, HS:] for a in at_v], axis=0))
+        q = jnp.concatenate([queries[i, :, lane] for i in places], axis=0)
+        s_vert = lax.dot_general(q, k_vert, over_keys, preferred_element_type=jnp.float32)
+        for n, i in enumerate(places):
+            at = [reach + i - slash[h, j] for j in range(ns)]
+            k_s = jnp.concatenate([window[a, :, :HS] for a in at], axis=0)
+            v_slash.append(jnp.concatenate([window[a, :, HS:] for a in at], axis=0))
+            rows = slice(n * BLK, (n + 1) * BLK)
+            s_s = lax.dot_general(q[rows], k_s, over_keys, preferred_element_type=jnp.float32)
+            scores.append((s_vert[rows], s_s, bv[i, pl.ds(h, 1), :], bs[i, pl.ds(h, 1), :]))
+    weights, totals = [], []
+    for s_v, s_s, b_v, b_s in scores:
+        s_v = s_v + b_v
+        s_s = jnp.concatenate([s_s[:, :BLK] + triangle, s_s[:, BLK:]], axis=1) + b_s
+        m = jnp.maximum(jnp.max(s_v, axis=1, keepdims=True), jnp.max(s_s, axis=1, keepdims=True))
+        w_v, w_s = jnp.exp2((s_v - m) * scale), jnp.exp2((s_s - m) * scale)
+        totals.append(jnp.sum(w_v, axis=1, keepdims=True) + jnp.sum(w_s, axis=1, keepdims=True))
+        weights.append((w_v.astype(jnp.bfloat16), w_s.astype(jnp.bfloat16)))
+    for n, lane in enumerate(lanes):
+        own = range(n * len(places), (n + 1) * len(places))
+        o_v = jnp.dot(
+            jnp.concatenate([weights[k][0] for k in own], axis=0), v_vert[n],
+            preferred_element_type=jnp.float32,
         )
-        s_s = s_s * scale + (bs[i, pl.ds(h, 1), :] + triangle)
-        s_v = s_vert[half * BLK : (half + 1) * BLK] * scale + bv[i, pl.ds(h, 1), :]
-        m = jnp.maximum(jnp.max(s_v, axis=1, keepdims=True), jnp.max(s_s, axis=1, keepdims=True))
-        w_v = jnp.exp(s_v - m)
-        w_s = jnp.exp(s_s - m)
-        totals.append(jnp.sum(w_v, axis=1, keepdims=True) + jnp.sum(w_s, axis=1, keepdims=True))
-        probs.append(w_v.astype(jnp.bfloat16))
-        outs.append(jnp.dot(w_s.astype(jnp.bfloat16), v_s, preferred_element_type=jnp.float32))
-    o_v = jnp.dot(jnp.concatenate(probs, axis=0), v_vert, preferred_element_type=jnp.float32)
-    o = (o_v + jnp.concatenate(outs, axis=0)) / jnp.concatenate(totals, axis=0)
-    o = o.astype(jnp.bfloat16)
-    out[0, :, lanes] = o[:BLK]
-    out[1, :, lanes] = o[BLK:]
+        for k, (slot, half) in zip(own, to):
+            o_s = jnp.dot(weights[k][1], v_slash[k], preferred_element_type=jnp.float32)
+            at = k - own[0]
+            o = (o_v[at * BLK : (at + 1) * BLK] + o_s) / totals[k]
+            att[slot, half, :, lane] = o.astype(jnp.bfloat16)
 
 
 def spread(values, copies, width):
@@ -68,7 +69,7 @@
 def layer_kernel(
     vertical, slash, vert_hbm, slash_hbm, q_hbm, k_hbm, v_hbm, w_hbm, out_ref,
     k_ref, v_ref, vert_v, slash_v, queries, pool, window, bv, bs, slots_v, slots, att, w,
-    to_sib, from_sib, to_cross, from_cross,
+    to_sib, from_sib, to_cross, from_cross, kept_back, held,
     in_sem, slot_sem, w_sem, sib_send, sib_recv, cross_send, cross_recv,
     lend_send, lend_recv, g_send, g_recv,
 ):
@@ -166,7 +167,7 @@
         for j in range(nv):
             v = vertical[h, j]
             second = jnp.where((vert // blocks == v // blocks) & (vert > v), 1, second)
-    slots_v[...] = second
+    slots_v[...] = 2 * (vert // blocks) + second
     place = pltpu.make_async_copy(slots_v, slots, slot_sem)
     place.start()
     vert_wide = spread(vert, nv, BLK)
@@ -237,7 +238,7 @@
         )
 
     def lend(n):
-        at = pl.ds(pl.multiple_of(n * PAIR * HS, PAIR * HS), PAIR * HS)
+        at = pl.ds(pl.multiple_of(n * TOGETHER * HS, TOGETHER * HS), TOGETHER * HS)
         return pltpu.make_async_remote_copy(
             src_ref=att.at[0, :, :, at],
             dst_ref=att.at[2, :, :, at],
@@ -247,62 +248,62 @@
             device_id_type=MESH,
         )
 
-    def attend(h, places, out):
-        attend_head(h, places, slots, vertical, slash, queries, pool, window, bv, bs, att.at[out])
-
-    def project(first, second, c):
-        rows = jnp.concatenate([att[first], att[second]], axis=0)
+    blocks_of_pool = pool.reshape(count * 2, BLK, 2 * HS)
+
+    def attend(n, places, to):
+        hs = [TOGETHER * n + k for k in range(TOGETHER)]
+        attend_heads(hs, places, slots, slash, queries, blocks_of_pool, window, bv, bs, att, to)
+
+    def project(parts, c):
+        rows = jnp.concatenate([att[a, b] for a, b in parts], axis=0)
         return jnp.dot(rows, w[c], preferred_element_type=jnp.float32)
 
-    @pl.loop(0, heads)
-    def _(h):
-        attend(h, (2 * corner + 1, 2 * cross + 1), 0)
-
-        @pl.when(h % PAIR == PAIR - 1)
-        def _():
-            lend(h // PAIR).start()
-
-    @pl.loop(0, heads)
-    def _(h):
-        attend(h, (2 * corner, 2 * cross), 1)
-
-    for n in range(heads // PAIR):
+    @pl.loop(0, heads // TOGETHER)
+    def _(n):
+        places = (2 * corner + 1, 2 * cross + 1, 2 * corner, 2 * cross)
+        attend(n, places, ((0, 0), (0, 1), (1, 0), (1, 1)))
+        lend(n).start()
+
+    for n in range(heads // TOGETHER):
         lend(n).wait_recv()
+
+    def pass_on(c):
+        hand(0, c).wait_recv()
+        part = kept_back[c % 2] + from_sib[0, c].astype(jnp.float32)
+        for half in range(2):
+            to_cross[c, half] = part[half * BLK : (half + 1) * BLK].astype(jnp.bfloat16)
+            over(half, c).start()
 
     @pl.loop(0, chunks)
     def _(c):
         weights(c).wait()
-        to_sib[0, c] = project((1, 0), (2, 0), c).astype(jnp.bfloat16)
+        part = project(((1, 0), (2, 0), (1, 1), (2, 1)), c)
+        to_sib[0, c] = part[: 2 * BLK].astype(jnp.bfloat16)
         hand(0, c).start()
+        kept_back[c % 2] = part[2 * BLK :]
+
+        @pl.when(c > 0)
+        def _():
+            pass_on(c - 1)
+
+    pass_on(chunks - 1)
+
+    @pl.loop(0, heads // TOGETHER)
+    def _(n):
+        places = (2 * sibling, 2 * sibling + 1, 2 * t, 2 * t + 1)
+        attend(n, places, ((3, 0), (3, 1), (4, 0), (4, 1)))
 
     @pl.loop(0, chunks)
     def _(c):
-        part = project((1, 1), (2, 1), c)
-        hand(0, c).wait_recv()
-        part = (part + from_sib[0, c].astype(jnp.float32)).astype(jnp.bfloat16)
-        to_cross[c, 0] = part[:BLK]
-        to_cross[c, 1] = part[BLK:]
-        over(0, c).start()
-        over(1, c).start()
-
-    @pl.loop(0, heads)
-    def _(h):
-        attend(h, (2 * sibling, 2 * sibling + 1), 3)
+        part = project(((3, 0), (3, 1), (4, 0), (4, 1)), c)
+        to_sib[1, c] = part[: 2 * BLK].astype(jnp.bfloat16)
+        hand(1, c).start()
+        held[c] = part[2 * BLK :]
 
     @pl.loop(0, chunks)
     def _(c):
-        to_sib[1, c] = project((3, 0), (3, 1), c).astype(jnp.bfloat16)
-        hand(1, c).start()
-
-    @pl.loop(0, heads)
-    def _(h):
-        attend(h, (2 * t, 2 * t + 1), 4)
-
-    @pl.loop(0, chunks)
-    def _(c):
-        part = project((4, 0), (4, 1), c)
         hand(1, c).wait_recv()
-        part = part + from_sib[1, c].astype(jnp.float32)
+        part = held[c] + from_sib[1, c].astype(jnp.float32)
         at = pl.ds(pl.multiple_of(c * WIDE, WIDE), WIDE)
         for half in range(2):
             over(half, c).wait_recv()
@@ -318,7 +319,7 @@
         over(0, c).wait_send()
         over(1, c).wait_send()
 
-    for n in range(heads // PAIR):
+    for n in range(heads // TOGETHER):
         lend(n).wait_send()
 
     for copy in sent + [near, far]:
@@ -358,6 +359,8 @@
             pltpu.VMEM((2, chunks) + part, jnp.bfloat16),
             pltpu.VMEM((chunks, 2, BLK, WIDE), jnp.bfloat16),
             pltpu.VMEM((chunks, 2, BLK, WIDE), jnp.bfloat16),
+            pltpu.VMEM((2,) + part, jnp.float32),
+            pltpu.VMEM((chunks,) + part, jnp.float32),
             dma((5,)),
             dma,
             dma((chunks,)),
@@ -365,8 +368,8 @@
             dma((2, chunks)),
             dma((2, chunks)),
             dma((2, chunks)),
-            dma((heads // PAIR,)),
-            dma((heads // PAIR,)),
+            dma((heads // TOGETHER,)),
+            dma((heads // TOGETHER,)),
             dma((17,)),
             dma((17,)),
         ],

time: 97.6 us -> 83.2 us (0.85)
  Pallas kernels: 94.3 us -> 79.6 us
    pallas_call x1, Pallas kernels: 94.3 us -> 79.6 us  [shards(): pl.pallas_call(layer_kernel, out_shape=jax.ShapeDtypeStruct((rows // 4, o...]
where the time goes in v5:
time: 83.2 us; the launch traced here: 82.7 us
  Pallas kernels  79.6 us (96%)
  local copies, waits for them, and re-layouts  3.1 us (4%)
    pallas_call x1, Pallas kernels, shards(): pl.pallas_call(layer_kernel, out_shape=jax.ShapeDtypeStruct((rows // 4, o...  79.6 us
    unnamed x1, local copies, waits for them, and re-layouts  3.1 us

profile of v5, /device:TPU:8, one launch (start us, length us, event | category | flops | bytes accessed | tf_op | source)
XLA Modules:
  0.0 82.7 jit_solution(11500629291744259370)
XLA Ops:
  0.0 79.6 %shard_map.64 = bf16[128,8192]{1,0:T(8,128)(2,1)} custom-call(s32[8,16]{1,0:T(8,128)} %vert_hbm.1, s32[8,8]{1,0:T(8,128)} %slash_hbm.1, s32[8,16]{1,0:T(8,128)} %vert_hbm.1, s32[8,8]{1,0:T(8,128)} %slash_hbm.1, bf16[8,64,1024]{2,1,0:T(8,128)(2,1)} %bitcast.3, bf16[8,64,128]{2,1,0:T(8,128)(2,1)} %bitcast.4, bf16[8,64,128]{2,1,0:T(8,128)(2,1)} %bitcast.5, ...), custom_call_target="tpu_custom_call" | custom-call | tf_op jit(solution)/shard_map/pallas_call | solution.py:339
  79.6 3.1 %copy.8 = bf16[128,8192]{1,0:T(8,128)(2,1)} copy(bf16[128,8192]{1,0:T(8,128)(2,1)} %shard_map.64) | data formatting | bytes 4194304

commit v6 on v5

--- a/solution.py
+++ b/solution.py
@@ -12,6 +12,8 @@
 WIDE = 1024
 NZ, NX, NY = 4, 2, 4
 TOGETHER = 2
+BEHIND = 3
+AHEAD = 1
 
 
 def attend_heads(hs, places, slots, slash, queries, pool, window, bv, bs, att, to):
@@ -121,9 +123,10 @@
     for h in range(heads):
         for j in range(nv):
             v = vertical[h, j]
-            mine = v // blocks == me
-            low = jnp.minimum(low, jnp.where(mine, v % blocks, blocks - 1))
-            high = jnp.maximum(high, jnp.where(mine, v % blocks, 0))
+            inside = v - me * blocks
+            mine = (inside >= 0) & (inside < blocks)
+            low = jnp.minimum(low, jnp.where(mine, inside, blocks - 1))
+            high = jnp.maximum(high, jnp.where(mine, inside, 0))
     inputs[0].wait()
     inputs[1].wait()
     for half, kv in enumerate((k_ref, v_ref)):
@@ -155,19 +158,44 @@
     send(0, pool.at[z, x, y], mirror)
     near = pltpu.make_async_remote_copy(
         src_ref=window.at[pl.ds(reach, blocks)], dst_ref=window.at[pl.ds(reach - blocks, blocks)],
-        send_sem=g_send.at[15], recv_sem=g_recv.at[15], device_id=after, device_id_type=MESH,
+        send_sem=g_send.at[25], recv_sem=g_recv.at[25], device_id=after, device_id_type=MESH,
     )
+
+    halves = (x, 1 - x)
+
+    def first(k):
+        for d in range(1, NY):
+            send(6 * k + d, pool.at[z, halves[k], y, 0], ctx(z, x, y + d))
+        for d in range(1, NZ):
+            send(6 * k + 3 + d, pool.at[z, halves[k], y, 1], ctx(z + d, x, y))
+
+    def second(k):
+        for d in range(1, NY):
+            got(6 * k + d, pool.at[z, halves[k], (y + NY - d) % NY, 0])
+        send(13 + 4 * k, pool.at[z, halves[k], :, 0], ctx(z + 1, x, y))
+        send(14 + 4 * k, pool.at[z, halves[k], :, 0], ctx(z + NZ - 1, x, y))
+        for d in range(1, NZ):
+            got(6 * k + 3 + d, pool.at[(z + NZ - d) % NZ, halves[k], y, 1])
+        send(15 + 4 * k, pool.at[:, halves[k], y, 1], ctx(z, x, y + 1))
+        send(16 + 4 * k, pool.at[:, halves[k], y, 1], ctx(z, x, y + NY - 1))
+
+    first(0)
+    got(0, pool.at[z, 1 - x, y])
+    first(1)
     near.start()
-
+    second(0)
+    second(1)
     for copy in inputs[2:]:
         copy.wait()
     vert = vert_v[...]
+    shard = vert >> (blocks.bit_length() - 1)
+    start = vert & ~(blocks - 1)
     second = jnp.zeros((heads, nv), jnp.int32)
     for h in range(heads):
         for j in range(nv):
             v = vertical[h, j]
-            second = jnp.where((vert // blocks == v // blocks) & (vert > v), 1, second)
-    slots_v[...] = 2 * (vert // blocks) + second
+            second = jnp.where((start <= v) & (v < vert), 1, second)
+    slots_v[...] = 2 * shard + second
     place = pltpu.make_async_copy(slots_v, slots, slot_sem)
     place.start()
     vert_wide = spread(vert, nv, BLK)
@@ -181,38 +209,29 @@
         bv[i] = jnp.where(kept, 0.0, NEG)
         bs[i] = jnp.where(slash_wide <= block, 0.0, NEG)
 
-    got(0, pool.at[z, 1 - x, y])
-    for d in range(1, NY):
-        send(d, pool.at[z, :, y, 0], ctx(z, x, y + d))
-    for d in range(1, NZ):
-        send(3 + d, pool.at[z, :, y, 1], ctx(z + d, x, y))
-    for d in range(1, NY):
-        got(d, pool.at[z, :, (y + NY - d) % NY, 0])
-    send(7, pool.at[z, :, :, 0], ctx(z + 1, x, y))
-    send(8, pool.at[z, :, :, 0], ctx(z + NZ - 1, x, y))
-    for d in range(1, NZ):
-        got(3 + d, pool.at[(z + NZ - d) % NZ, :, y, 1])
-    send(9, pool.at[:, :, y, 1], ctx(z, x, y + 1))
-    send(10, pool.at[:, :, y, 1], ctx(z, x, y + NY - 1))
     near.wait_recv()
     far = pltpu.make_async_remote_copy(
         src_ref=window.at[pl.ds(reach - blocks + 1, blocks - 1)],
         dst_ref=window.at[pl.ds(reach - 2 * blocks + 1, blocks - 1)],
-        send_sem=g_send.at[16], recv_sem=g_recv.at[16], device_id=after, device_id_type=MESH,
+        send_sem=g_send.at[26], recv_sem=g_recv.at[26], device_id=after, device_id_type=MESH,
     )
     far.start()
-    got(7, pool.at[down, :, :, 0])
-    send(11, pool.at[down, 0, :, 0], ctx(z + 1, x, y))
-    got(8, pool.at[up, :, :, 0])
-    send(12, pool.at[up, 1, :, 0], ctx(z + NZ - 1, x, y))
-    got(9, pool.at[:, :, left, 1])
-    send(13, pool.at[:, 0, left, 1], ctx(z, x, y + 1))
-    got(10, pool.at[:, :, right, 1])
-    send(14, pool.at[:, 1, right, 1], ctx(z, x, y + NY - 1))
-    got(11, pool.at[(z + 2) % NZ, 0, :, 0])
-    got(12, pool.at[(z + 2) % NZ, 1, :, 0])
-    got(13, pool.at[:, 0, (y + 2) % NY, 1])
-    got(14, pool.at[:, 1, (y + 2) % NY, 1])
+    got(13, pool.at[down, x, :, 0])
+    send(21, pool.at[down, x, :, 0], ctx(z + 1, x, y))
+    got(15, pool.at[:, x, left, 1])
+    send(23, pool.at[:, x, left, 1], ctx(z, x, y + 1))
+    got(18, pool.at[up, 1 - x, :, 0])
+    send(22, pool.at[up, 1 - x, :, 0], ctx(z + NZ - 1, x, y))
+    got(20, pool.at[:, 1 - x, right, 1])
+    send(24, pool.at[:, 1 - x, right, 1], ctx(z, x, y + NY - 1))
+    got(16, pool.at[:, x, right, 1])
+    got(19, pool.at[:, 1 - x, left, 1])
+    got(14, pool.at[up, x, :, 0])
+    got(17, pool.at[down, 1 - x, :, 0])
+    got(21, pool.at[(z + 2) % NZ, x, :, 0])
+    got(22, pool.at[(z + 2) % NZ, 1 - x, :, 0])
+    got(23, pool.at[:, x, (y + 2) % NY, 1])
+    got(24, pool.at[:, 1 - x, (y + 2) % NY, 1])
     far.wait_recv()
     place.wait()
 
@@ -264,12 +283,20 @@
         attend(n, places, ((0, 0), (0, 1), (1, 0), (1, 1)))
         lend(n).start()
 
+    def attend_here(n):
+        places = (2 * sibling, 2 * sibling + 1, 2 * t, 2 * t + 1)
+        attend(n, places, ((3, 0), (3, 1), (4, 0), (4, 1)))
+
+    @pl.loop(0, AHEAD)
+    def _(n):
+        attend_here(n)
+
     for n in range(heads // TOGETHER):
         lend(n).wait_recv()
 
     def pass_on(c):
         hand(0, c).wait_recv()
-        part = kept_back[c % 2] + from_sib[0, c].astype(jnp.float32)
+        part = kept_back[c % BEHIND] + from_sib[0, c].astype(jnp.float32)
         for half in range(2):
             to_cross[c, half] = part[half * BLK : (half + 1) * BLK].astype(jnp.bfloat16)
             over(half, c).start()
@@ -280,18 +307,20 @@
         part = project(((1, 0), (2, 0), (1, 1), (2, 1)), c)
         to_sib[0, c] = part[: 2 * BLK].astype(jnp.bfloat16)
         hand(0, c).start()
-        kept_back[c % 2] = part[2 * BLK :]
-
-        @pl.when(c > 0)
+
+        @pl.when(c >= BEHIND)
         def _():
-            pass_on(c - 1)
-
-    pass_on(chunks - 1)
-
-    @pl.loop(0, heads // TOGETHER)
+            pass_on(c - BEHIND)
+
+        kept_back[c % BEHIND] = part[2 * BLK :]
+
+    @pl.loop(chunks - BEHIND, chunks)
+    def _(c):
+        pass_on(c)
+
+    @pl.loop(AHEAD, heads // TOGETHER)
     def _(n):
-        places = (2 * sibling, 2 * sibling + 1, 2 * t, 2 * t + 1)
-        attend(n, places, ((3, 0), (3, 1), (4, 0), (4, 1)))
+        attend_here(n)
 
     @pl.loop(0, chunks)
     def _(c):
@@ -359,7 +388,7 @@
             pltpu.VMEM((2, chunks) + part, jnp.bfloat16),
             pltpu.VMEM((chunks, 2, BLK, WIDE), jnp.bfloat16),
             pltpu.VMEM((chunks, 2, BLK, WIDE), jnp.bfloat16),
-            pltpu.VMEM((2,) + part, jnp.float32),
+            pltpu.VMEM((BEHIND,) + part, jnp.float32),
             pltpu.VMEM((chunks,) + part, jnp.float32),
             dma((5,)),
             dma,
@@ -370,8 +399,8 @@
             dma((2, chunks)),
             dma((heads // TOGETHER,)),
             dma((heads // TOGETHER,)),
-            dma((17,)),
-            dma((17,)),
+            dma((27,)),
+            dma((27,)),
         ],
         compiler_params=pltpu.CompilerParams(
             collective_id=0, has_side_effects=True, vmem_limit_bytes=60 << 20

time: 83.2 us -> 78.1 us (0.939)
  Pallas kernels: 79.6 us -> 73.8 us
    pallas_call x1, Pallas kernels: 79.6 us -> 73.8 us  [shards(): pl.pallas_call(layer_kernel, out_shape=jax.ShapeDtypeStruct((rows // 4, o...]
where the time goes in v6:
time: 78.1 us; the launch traced here: 76.9 us
  Pallas kernels  73.8 us (94%)
  local copies, waits for them, and re-layouts  3.1 us (4%)
    pallas_call x1, Pallas kernels, shards(): pl.pallas_call(layer_kernel, out_shape=jax.ShapeDtypeStruct((rows // 4, o...  73.8 us
    unnamed x1, local copies, waits for them, and re-layouts  3.1 us

profile of v6, /device:TPU:8, one launch (start us, length us, event | category | flops | bytes accessed | tf_op | source)
XLA Modules:
  0.0 76.9 jit_solution(16657199744542782516)
XLA Ops:
  0.0 73.8 %shard_map.64 = bf16[128,8192]{1,0:T(8,128)(2,1)} custom-call(s32[8,16]{1,0:T(8,128)} %vert_hbm.1, s32[8,8]{1,0:T(8,128)} %slash_hbm.1, s32[8,16]{1,0:T(8,128)} %vert_hbm.1, s32[8,8]{1,0:T(8,128)} %slash_hbm.1, bf16[8,64,1024]{2,1,0:T(8,128)(2,1)} %bitcast.3, bf16[8,64,128]{2,1,0:T(8,128)(2,1)} %bitcast.4, bf16[8,64,128]{2,1,0:T(8,128)(2,1)} %bitcast.5, ...), custom_call_target="tpu_custom_call" | custom-call | tf_op jit(solution)/shard_map/pallas_call | solution.py:368
  73.8 3.1 %copy.8 = bf16[128,8192]{1,0:T(8,128)(2,1)} copy(bf16[128,8192]{1,0:T(8,128)(2,1)} %shard_map.64) | data formatting | bytes 4194304

commit v7 on v6

--- a/solution.py
+++ b/solution.py
@@ -69,10 +69,10 @@
 
 
 def layer_kernel(
-    vertical, slash, vert_hbm, slash_hbm, q_hbm, k_hbm, v_hbm, w_hbm, out_ref,
+    vertical, slash, vert_hbm, slash_hbm, q_hbm, k_hbm, v_hbm, w_hbm, out_hbm,
     k_ref, v_ref, vert_v, slash_v, queries, pool, window, bv, bs, slots_v, slots, att, w,
-    to_sib, from_sib, to_cross, from_cross, kept_back, held,
-    in_sem, slot_sem, w_sem, sib_send, sib_recv, cross_send, cross_recv,
+    to_sib, from_sib, to_cross, from_cross, kept_back, held, done,
+    done_sem, in_sem, slot_sem, w_sem, sib_send, sib_recv, cross_send, cross_recv,
     lend_send, lend_recv, g_send, g_recv,
 ):
     heads, nv = vertical.shape
@@ -180,9 +180,9 @@
         send(16 + 4 * k, pool.at[:, halves[k], y, 1], ctx(z, x, y + NY - 1))
 
     first(0)
+    near.start()
     got(0, pool.at[z, 1 - x, y])
     first(1)
-    near.start()
     second(0)
     second(1)
     for copy in inputs[2:]:
@@ -273,6 +273,10 @@
         hs = [TOGETHER * n + k for k in range(TOGETHER)]
         attend_heads(hs, places, slots, slash, queries, blocks_of_pool, window, bv, bs, att, to)
 
+    def finish(c):
+        at = pl.ds(pl.multiple_of(c * WIDE, WIDE), WIDE)
+        return pltpu.make_async_copy(done.at[c], out_hbm.at[:, at], done_sem.at[c])
+
     def project(parts, c):
         rows = jnp.concatenate([att[a, b] for a, b in parts], axis=0)
         return jnp.dot(rows, w[c], preferred_element_type=jnp.float32)
@@ -333,18 +337,19 @@
     def _(c):
         hand(1, c).wait_recv()
         part = held[c] + from_sib[1, c].astype(jnp.float32)
-        at = pl.ds(pl.multiple_of(c * WIDE, WIDE), WIDE)
         for half in range(2):
             over(half, c).wait_recv()
             here = part[half * BLK : (half + 1) * BLK]
-            out_ref[half * BLK : (half + 1) * BLK, at] = (
+            done[c, half * BLK : (half + 1) * BLK] = (
                 here + from_cross[c, half].astype(jnp.float32)
             ).astype(jnp.bfloat16)
+        finish(c).start()
 
     @pl.loop(0, chunks)
     def _(c):
         hand(0, c).wait_send()
         hand(1, c).wait_send()
+        finish(c).wait()
         over(0, c).wait_send()
         over(1, c).wait_send()
 
@@ -362,14 +367,13 @@
     blocks = rows // BLK
     chunks = out_weight.shape[1] // WIDE
     part = (rows // 4, WIDE)
-    vmem = pl.BlockSpec(memory_space=pltpu.VMEM)
     smem = pl.BlockSpec(memory_space=pltpu.SMEM)
     dma = pltpu.SemaphoreType.DMA
     return pl.pallas_call(
         layer_kernel,
         out_shape=jax.ShapeDtypeStruct((rows // 4, out_weight.shape[1]), jnp.bfloat16),
         in_specs=[smem, smem] + [pl.BlockSpec(memory_space=pltpu.HBM)] * 6,
-        out_specs=vmem,
+        out_specs=pl.BlockSpec(memory_space=pltpu.HBM),
         scratch_shapes=[
             pltpu.VMEM((blocks, BLK, HS), jnp.bfloat16),
             pltpu.VMEM((blocks, BLK, HS), jnp.bfloat16),
@@ -390,6 +394,8 @@
             pltpu.VMEM((chunks, 2, BLK, WIDE), jnp.bfloat16),
             pltpu.VMEM((BEHIND,) + part, jnp.float32),
             pltpu.VMEM((chunks,) + part, jnp.float32),
+            pltpu.VMEM((chunks,) + part, jnp.bfloat16),
+            dma((chunks,)),
             dma((5,)),
             dma,
             dma((chunks,)),

time: 78.1 us -> 76.5 us (0.980)
  Pallas kernels: 73.8 us -> 72.3 us
    pallas_call x1, Pallas kernels: 73.8 us -> 72.3 us  [shards(): pl.pallas_call(layer_kernel, out_shape=jax.ShapeDtypeStruct((rows // 4, o...]
where the time goes in v7:
time: 76.5 us; the launch traced here: 75.4 us
  Pallas kernels  72.3 us (95%)
  local copies, waits for them, and re-layouts  3.1 us (4%)
    pallas_call x1, Pallas kernels, shards(): pl.pallas_call(layer_kernel, out_shape=jax.ShapeDtypeStruct((rows // 4, o...  72.3 us
    unnamed x1, local copies, waits for them, and re-layouts  3.1 us

profile of v7, /device:TPU:8, one launch (start us, length us, event | category | flops | bytes accessed | tf_op | source)
XLA Modules:
  0.0 75.4 jit_solution(9724011658538725782)
XLA Ops:
  0.0 72.3 %shard_map.64 = bf16[128,8192]{1,0:T(8,128)(2,1)} custom-call(s32[8,16]{1,0:T(8,128)} %vert_hbm.1, s32[8,8]{1,0:T(8,128)} %slash_hbm.1, s32[8,16]{1,0:T(8,128)} %vert_hbm.1, s32[8,8]{1,0:T(8,128)} %slash_hbm.1, bf16[8,64,1024]{2,1,0:T(8,128)(2,1)} %bitcast.3, bf16[8,64,128]{2,1,0:T(8,128)(2,1)} %bitcast.4, bf16[8,64,128]{2,1,0:T(8,128)(2,1)} %bitcast.5, ...), custom_call_target="tpu_custom_call" | custom-call | tf_op jit(solution)/shard_map/pallas_call | solution.py:372
  72.3 3.1 %copy.8 = bf16[128,8192]{1,0:T(8,128)(2,1)} copy(bf16[128,8192]{1,0:T(8,128)(2,1)} %shard_map.64) | data formatting | bytes 4194304

commit v8 on v7

--- a/solution.py
+++ b/solution.py
@@ -13,7 +13,7 @@
 NZ, NX, NY = 4, 2, 4
 TOGETHER = 2
 BEHIND = 3
-AHEAD = 1
+AHEAD = 0
 
 
 def attend_heads(hs, places, slots, slash, queries, pool, window, bv, bs, att, to):

time: 76.5 us -> 76.4 us (level)
  no operation moved by 1% of the time
where the time goes in v8:
time: 76.4 us; the launch traced here: 75.4 us
  Pallas kernels  72.3 us (95%)
  local copies, waits for them, and re-layouts  3.1 us (4%)
    pallas_call x1, Pallas kernels, shards(): pl.pallas_call(layer_kernel, out_shape=jax.ShapeDtypeStruct((rows // 4, o...  72.3 us
    unnamed x1, local copies, waits for them, and re-layouts  3.1 us

profile of v8, /device:TPU:8, one launch (start us, length us, event | category | flops | bytes accessed | tf_op | source)
XLA Modules:
  0.0 75.4 jit_solution(14956139730208994901)
XLA Ops:
  0.0 72.3 %shard_map.64 = bf16[128,8192]{1,0:T(8,128)(2,1)} custom-call(s32[8,16]{1,0:T(8,128)} %vert_hbm.1, s32[8,8]{1,0:T(8,128)} %slash_hbm.1, s32[8,16]{1,0:T(8,128)} %vert_hbm.1, s32[8,8]{1,0:T(8,128)} %slash_hbm.1, bf16[8,64,1024]{2,1,0:T(8,128)(2,1)} %bitcast.3, bf16[8,64,128]{2,1,0:T(8,128)(2,1)} %bitcast.4, bf16[8,64,128]{2,1,0:T(8,128)(2,1)} %bitcast.5, ...), custom_call_target="tpu_custom_call" | custom-call | tf_op jit(solution)/shard_map/pallas_call | solution.py:372
  72.3 3.1 %copy.8 = bf16[128,8192]{1,0:T(8,128)(2,1)} copy(bf16[128,8192]{1,0:T(8,128)(2,1)} %shard_map.64) | data formatting | bytes 4194304
